TPU v7x, 256 devices: a whole 4x4x8 slice. The times are simulated.
256 devices in a mesh: line: 8 (over x, core), span: 32 (over y, z).
Axes of the slice: x: 4, y: 4, z: 8, core: 2. Of those that a mesh axis runs over, the one named last changes fastest.
Arguments:
- residual: float32 [128, 16, 64, 320], P('span', 'line'), may hold values from -6 to 6
- previous: float32 [128, 16, 64, 320], P('span', 'line'), may hold values from -6 to 6
- pivot_inverse: float32 [128, 16, 320, 320], P('span', 'line')
- lower_blocks: float32 [128, 16, 320, 320], P('span', 'line')
- upper_blocks: float32 [128, 16, 320, 320], P('span', 'line')
- flux_jacobian: float32 [128, 16, 80, 320], P('span', 'line'), may hold values from -0.625 to 0.625
- trace_operator: float32 [320, 320], replicated, may hold values from -0.3125 to 0.3125
- lift_operator: float32 [320, 320], replicated, may hold values from -0.3125 to 0.3125
- lengths: int32 [128], P('span'), may hold values from 8 to 16, as said below
- neighbour_line: int32 [128, 4], P('span'), may hold values from 0 to 127, as said below
- neighbour_face: int32 [128, 4], P('span'), may hold values from 0 to 3
Outputs:
- update: float32 [128, 16, 64, 320], P('span', 'line')
Inputs may be any that keep to these rules, and one draw needn't show every extreme that they name: `lengths`: every line has between 8 and 16 elements; some line has 16 and some line 16 // 2. `neighbour_line`: no line is its own neighbour; neighbours may lie anywhere in the span numbering.
All inputs are finite; a program needn't handle non-finite values.
Results may differ from a plain program's by a relative error of at most 0.0001.
Values sent between devices are 32-bit elements; how exact they have to be, the bound alone decides.
No kernel may reach another device: no remote copies, remote signals or barrier semaphores. Data moves between devices by JAX's collectives and lax.ppermute only.
A program may use at most 192 MiB of HBM per device.

v0:
```python
import jax
import jax.numpy as jnp
from jax import lax
from jax.experimental import pallas as pl
from jax.experimental.pallas import tpu as pltpu
from jax.sharding import PartitionSpec as P


NB = 320
NF = 80
FACES = 4
NV = 64
ROW = 128
YS, ZS = 4, 8
LINE_ROWS = 4
SLOTS = LINE_ROWS * FACES
HALF = SLOTS // 2


VMEM = pl.BlockSpec(memory_space=pltpu.VMEM)
SMEM = pl.BlockSpec(memory_space=pltpu.SMEM)


def f32(*shape):
    return jax.ShapeDtypeStruct(shape, jnp.float32)


def z_shift(array, by):
    pairs = [(y * ZS + z, y * ZS + (z + by) % ZS) for y in range(YS) for z in range(ZS)]
    return lax.ppermute(array, "span", pairs)


def y_shift(array, by):
    pairs = [(y * ZS + z, (y + by) % YS * ZS + z) for y in range(YS) for z in range(ZS)]
    return lax.ppermute(array, "span", pairs)


def y_shift_cross(array, by):
    spans = YS * ZS
    pairs = [
        (i * spans + y * ZS + z, (i ^ 1) * spans + (y + by) % YS * ZS + z)
        for i in range(8)
        for y in range(YS)
        for z in range(ZS)
    ]
    return lax.ppermute(array, ("line", "span"), pairs)


def core_swap(array):
    return lax.ppermute(array, "line", [(i, i ^ 1) for i in range(8)])


def chip_shift(array, by, chips=range(4)):
    pairs = [
        (2 * x + core, 2 * (x + by) + core)
        for x in chips
        for core in range(2)
        if 0 <= x + by < 4
    ]
    return lax.ppermute(array, "line", pairs)


def high_low(array):
    high = lax.reduce_precision(array, 8, 7)
    return high.astype(jnp.bfloat16), (array - high).astype(jnp.bfloat16)


def split_value(x):
    high = x.astype(jnp.bfloat16)
    return high, (x - high.astype(jnp.float32)).astype(jnp.bfloat16)


def product(w_high, w_low, x_high, x_both):
    wide = jnp.dot(w_high, x_both, preferred_element_type=jnp.float32)
    low = jnp.dot(w_low, x_high, preferred_element_type=jnp.float32)
    return wide[:, :ROW] + wide[:, ROW:] + low


def left_lanes():
    return lax.broadcasted_iota(jnp.int32, (NB, ROW), 1) < NV


def apply_pair(w_high, w_low, first, second, x):
    high, low = split_value(x)
    both = jnp.concatenate([high, low], axis=1)
    left = product(w_high[first], w_low[first], high, both)
    right = product(w_high[second], w_low[second], high, both)
    return jnp.where(left_lanes(), left, right)


def pick_kernel(parts):
    def kernel(table, place, own, up1, up2, up3, down1, down2, down3, up4, down4, *refs):
        y, z, core = place[0], place[1], place[2]
        whole = ((0, own), (7, up1), (6, up2), (5, up3), (1, down1), (2, down2), (3, down3))
        relays, outs = list(refs[: -len(parts)]), refs[-len(parts) :]
        for out, (dy, other, relayed) in zip(outs, parts):
            first = (1 - core if other else core) * HALF
            relay = relays.pop(0) if relayed else None

            def body(i, carry):
                asked = table[dy, first + i]
                owner, piece = asked // SLOTS, asked % SLOTS
                dz = (owner % ZS - z + ZS) % ZS

                @pl.when(owner // ZS == y)
                def _():
                    for k, source in whole:
                        @pl.when(dz == k)
                        def _():
                            out[i] = source[piece]

                    @pl.when((dz == 4) & (piece < HALF))
                    def _():
                        out[i] = up4[jnp.minimum(piece, HALF - 1)]

                    @pl.when((dz == 4) & (piece >= HALF))
                    def _():
                        out[i] = down4[jnp.maximum(piece - HALF, 0)]

                if relayed:
                    @pl.when(owner // ZS == (y + relayed) % YS)
                    def _():
                        out[i] = relay[i]

                return carry

            lax.fori_loop(0, HALF, body, 0)

    return kernel


def halves_kernel(up, down, up_half, down_half):
    up_half[...] = up[:HALF]
    down_half[...] = down[HALF:]


def whole_product(left, right_high, right_low):
    high, low = split_value(left)
    total = jnp.dot(high, right_high, preferred_element_type=jnp.float32)
    total += jnp.dot(low, right_high, preferred_element_type=jnp.float32)
    return total + jnp.dot(high, right_low, preferred_element_type=jnp.float32)


def own_kernel(core, kept, came, given_kept, given_came, high, low, own):
    first = core[0] == 0
    across = (((1,), (1,)), ((), ()))
    for half in range(2):
        blocks = (kept, came) if half == 0 else (came, kept)
        given = (given_kept, given_came) if half == 0 else (given_came, given_kept)
        values = []
        for element in range(2):
            block = jnp.where(first, blocks[0][0, element], blocks[1][0, element])
            w_high, w_low = split_value(block)
            high[0, 2 * half + element], low[0, 2 * half + element] = w_high, w_low
            x_high, x_low = split_value(jnp.where(first, given[0][0, element], given[1][0, element]))
            value = lax.dot_general(w_high, x_high, across, preferred_element_type=jnp.float32)
            value += lax.dot_general(w_high, x_low, across, preferred_element_type=jnp.float32)
            value += lax.dot_general(w_low, x_high, across, preferred_element_type=jnp.float32)
            values.append(value)
        own[0, half] = jnp.concatenate(values, axis=1)


def chain_kernel(order):
    def kernel(core, alive, kept, came, high, low, total):
        first = core[0] == 0
        for element in range(4):
            pair = (kept, came) if element < 2 else (came, kept)
            block = jnp.where(first, pair[0][0, element % 2], pair[1][0, element % 2])
            high[0, element], low[0, element] = split_value(block)
            if element == order[0]:
                start = block
        value = start
        for element in order[1:]:
            value = whole_product(value, high[0, element], low[0, element])
        total[0] = value * alive[pl.program_id(0), 3]

    return kernel


def alive_lanes(alive, element):
    lane = lax.broadcasted_iota(jnp.int32, (1, ROW), 1)
    return jnp.where(lane < NV, alive[0, element], alive[1, element])


def forward_kernel(table, place, alive, mine, below, above, mine_cross, below_cross, above_cross,
                   jacobian, jacobian_came, lift_high, lift_low, pivot_high, pivot_low, own,
                   l_high, l_low, out, last, held, terms):
    y, core = place[0], place[2]
    left = left_lanes()
    row = lax.broadcasted_iota(jnp.int32, (NB, NB), 0) // NF
    column = lax.broadcasted_iota(jnp.int32, (NB, NB), 1) // NF
    own_face = row == column

    def line_step(line, carry):
        for cross in range(2):
            half = 1 - core if cross else core
            here, down, up = (mine_cross, below_cross, above_cross) if cross else (mine, below, above)
            source = jacobian_came if cross else jacobian
            for face in range(FACES):
                slot = line * FACES + face
                dy = (table[0, core * HALF + slot] // (SLOTS * ZS) - y + YS) % YS
                from_below = (dy == 3) if cross else (dy >= 2)
                value = jnp.where(from_below, down[slot], up[slot])
                held[pl.ds(face * NF, NF), :] = jnp.where(dy == 0, here[slot], value)
            high, low = split_value(held[...])
            both = jnp.concatenate([high, low], axis=1)
            fluxes = []
            for element in range(2):
                tiled = jnp.concatenate([source[core * 2 + line, element]] * FACES, axis=0)
                wide = split_value(jnp.where(own_face, tiled, 0.0))
                fluxes.append(product(*wide, high, both))
            high, low = split_value(jnp.where(left, *fluxes))
            both = jnp.concatenate([high, low], axis=1)
            term = product(lift_high[...], lift_low[...], high, both)
            first = 4 * line + 2 * half
            term = apply_pair(pivot_high, pivot_low, first, first + 1, term)
            terms[line, half] = own[line, half] - term
        return carry

    lax.fori_loop(0, 2, line_step, 0)
    for half in range(2):
        first, second = terms[0, half], terms[1, half]
        out[2 * half] = jnp.where(left, first, pltpu.roll(second, NV, 1))
        out[2 * half + 1] = jnp.where(left, pltpu.roll(first, NV, 1), second)
    last[...] = out[0] * alive_lanes(alive, 0)

    def step(element, carry):
        term = apply_pair(l_high, l_low, element, 4 + element, last[...])
        last[...] = (out[element] + term) * alive_lanes(alive, element)
        return carry

    lax.fori_loop(1, 4, step, 0)


def enter(near, mid, far, close, apart):
    value = mid[...] + apply_pair(*apart, 0, 1, far[...])
    return near[...] + apply_pair(*close, 0, 1, value)


def split_blocks(source, high, low):
    for line in range(2):
        high[line], low[line] = split_value(source[line])


def middle_kernel(alive, near, mid, far, close, apart, driving,
                  l_high, l_low, u_high, u_low, sweep, first, *split):
    split_blocks(close, *split[:2])
    split_blocks(apart, *split[2:])
    first[...] = enter(near, mid, far, split[:2], split[2:])

    def up(element, carry):
        term = apply_pair(l_high, l_low, element, 4 + element, first[...])
        first[...] = (driving[element] + term) * alive_lanes(alive, element)
        sweep[element] = first[...]
        return carry

    lax.fori_loop(0, 4, up, 0)

    def down(step, carry):
        element = 2 - step
        term = apply_pair(u_high, u_low, element, 4 + element, first[...])
        first[...] = (sweep[element] + term) * alive_lanes(alive, element)
        return carry

    lax.fori_loop(0, 3, down, 0)


def backward_kernel(core, alive, near, mid, far, close, apart, sweep,
                    u_high, u_low, kept, sent, held, *split):
    split_blocks(close, *split[:2])
    split_blocks(apart, *split[2:])
    held[...] = enter(near, mid, far, split[:2], split[2:])

    def down(step, carry):
        element = 3 - step
        term = apply_pair(u_high, u_low, element, 4 + element, held[...])
        value = (sweep[element] + term) * alive_lanes(alive, element)
        held[...] = value
        natural = jnp.transpose(value)

        @pl.when(element // 2 == core[0])
        def _():
            kept[0, element % 2] = natural[:NV]
            kept[1, element % 2] = natural[NV:]

        @pl.when(element // 2 != core[0])
        def _():
            sent[0, element % 2] = natural[:NV]
            sent[1, element % 2] = natural[NV:]

        return carry

    lax.fori_loop(0, 4, down, 0)


def call(kernel, specs, out_shape, operands, flops, scratch=(), mib=16):
    out_specs = jax.tree.map(lambda _: VMEM, out_shape)
    moved = sum(4 * o.size for o in jax.tree.leaves((operands, out_shape)))
    return pl.pallas_call(
        kernel,
        out_shape=out_shape,
        in_specs=specs,
        out_specs=out_specs,
        scratch_shapes=list(scratch),
        compiler_params=pltpu.CompilerParams(vmem_limit_bytes=mib << 20),
        cost_estimate=pl.CostEstimate(flops=flops, bytes_accessed=moved, transcendentals=0),
    )(*operands)


def local(
    residual,
    previous,
    pivot_inverse,
    lower_blocks,
    upper_blocks,
    flux_jacobian,
    trace_operator,
    lift_operator,
    lengths,
    neighbour_line,
    neighbour_face,
):
    high = lax.Precision.HIGH
    line_pos = lax.axis_index("line")
    span_pos = lax.axis_index("span")
    core = line_pos % 2
    elements = residual.shape[1]
    position = line_pos * elements + jnp.arange(elements, dtype=jnp.int32)
    live = (position[None, :] < lengths[:, None]).astype(jnp.float32)
    place = jnp.stack([span_pos // ZS, span_pos % ZS, core]).astype(jnp.int32)
    core_ref = core.astype(jnp.int32).reshape(1)

    masked = (previous * live[:, :, None, None]).reshape(LINE_ROWS, ROW, NB)
    own = jnp.einsum("lmn,nk->lkm", masked, trace_operator, precision=high)
    own = own.reshape(SLOTS, NF, ROW)

    chip_position = line_pos // 2 * 4 + jnp.arange(4, dtype=jnp.int32)
    chip_lengths = lax.dynamic_slice_in_dim(lengths, core * 2, 2, 0)
    alive = (chip_position[None, :] < chip_lengths[:, None]).astype(jnp.float32)
    block = (1, 2, NB, NB)

    def chip_chain(blocks, came, order):
        split_shape = jax.ShapeDtypeStruct((2, 4, NB, NB), jnp.bfloat16)
        split_spec = pl.BlockSpec((1, 4, NB, NB), lambda i, core, alive: (i, 0, 0, 0))
        split_high, split_low, total = pl.pallas_call(
            chain_kernel(order),
            name="chain",
            grid_spec=pltpu.PrefetchScalarGridSpec(
                num_scalar_prefetch=2,
                grid=(2,),
                in_specs=[
                    pl.BlockSpec(block, lambda i, core, alive: (core[0] * 2 + i, 0, 0, 0)),
                    pl.BlockSpec(block, lambda i, core, alive: (core[0] * 2 + i, 0, 0, 0)),
                ],
                out_specs=[
                    split_spec,
                    split_spec,
                    pl.BlockSpec((1, NB, NB), lambda i, core, alive: (i, 0, 0)),
                ],
            ),
            out_shape=[split_shape, split_shape, f32(2, NB, NB)],
            compiler_params=pltpu.CompilerParams(vmem_limit_bytes=60 << 20),
            cost_estimate=pl.CostEstimate(
                flops=36 * NB**3, bytes_accessed=32 * NB * NB, transcendentals=0
            ),
        )(core_ref, alive, blocks, came)
        return (split_high.reshape(8, NB, NB), split_low.reshape(8, NB, NB)), total

    def pivot_parts(came, given_came):
        split_shape = jax.ShapeDtypeStruct((2, 4, NB, NB), jnp.bfloat16)
        split_spec = pl.BlockSpec((1, 4, NB, NB), lambda i, core: (i, 0, 0, 0))
        spec = pl.BlockSpec(block, lambda i, core: (core[0] * 2 + i, 0, 0, 0))
        given = pl.BlockSpec((1, 2, NV, NB), lambda i, core: (core[0] * 2 + i, 0, 0, 0))
        high, low, own = pl.pallas_call(
            own_kernel,
            name="own",
            grid_spec=pltpu.PrefetchScalarGridSpec(
                num_scalar_prefetch=1,
                grid=(2,),
                in_specs=[spec, spec, given, given],
                out_specs=[
                    split_spec,
                    split_spec,
                    pl.BlockSpec((1, 2, NB, ROW), lambda i, core: (i, 0, 0, 0)),
                ],
            ),
            out_shape=[split_shape, split_shape, f32(2, 2, NB, ROW)],
            compiler_params=pltpu.CompilerParams(vmem_limit_bytes=60 << 20),
            cost_estimate=pl.CostEstimate(
                flops=48 * NB * NB * NV, bytes_accessed=64 * NB * NB, transcendentals=0
            ),
        )(core_ref, pivot_inverse, came, residual, given_came)
        return high.reshape(8, NB, NB), low.reshape(8, NB, NB), own

    (own, residual, pivot_inverse, lower_blocks, upper_blocks, flux_jacobian, lift_operator,
     neighbour_line, neighbour_face) = lax.optimization_barrier(
        (own, residual, pivot_inverse, lower_blocks, upper_blocks, flux_jacobian, lift_operator,
         neighbour_line, neighbour_face)
    )
    up1 = z_shift(own, 1)
    down1 = z_shift(own, -1)
    lower_came = core_swap(lower_blocks)
    upper_came = core_swap(upper_blocks)
    lift = high_low(lift_operator.T)
    l_split, up_all = chip_chain(lower_blocks, lower_came, (3, 2, 1, 0))
    asked = (neighbour_line * FACES + neighbour_face).reshape(1, SLOTS)
    table = jnp.concatenate([asked, y_shift(asked, -1)])
    up1, down1, l_split, up_all, upper_came, table, lift = lax.optimization_barrier(
        (up1, down1, l_split, up_all, upper_came, table, lift)
    )
    up2 = z_shift(up1, 1)
    down2 = z_shift(down1, -1)
    m1 = chip_shift(up_all, 1, (1, 2))
    m2 = chip_shift(up_all, 2, (1,))
    pivot_came = core_swap(pivot_inverse)
    residual_came = core_swap(residual)
    jacobian_came = core_swap(flux_jacobian)
    u_split, down_all = chip_chain(upper_blocks, upper_came, (0, 1, 2, 3))
    n1 = chip_shift(down_all, -1, (2, 1))
    n2 = chip_shift(down_all, -2, (2,))
    up2, down2, u_split, down_all, pivot_came, residual_came, jacobian_came = (
        lax.optimization_barrier(
            (up2, down2, u_split, down_all, pivot_came, residual_came, jacobian_came)
        )
    )
    up3 = z_shift(up2, 1)
    down3 = z_shift(down2, -1)
    pivot = pivot_parts(pivot_came, residual_came)
    table = jnp.concatenate([table, y_shift(table, 2)])
    up3, down3, table, pivot = lax.optimization_barrier((up3, down3, table, pivot))
    up_half, down_half = call(
        halves_kernel, [VMEM] * 2, [f32(HALF, NF, ROW)] * 2, (up3, down3), 0, mib=4
    )
    up4 = z_shift(up_half, 1)
    down4 = z_shift(down_half, -1)

    def pick(parts, relays=()):
        return call(
            pick_kernel(parts), [SMEM] * 2 + [VMEM] * (9 + len(relays)),
            [f32(HALF, NF, ROW)] * len(parts),
            (table, place, own, up1, up2, up3, down1, down2, down3, up4, down4, *relays),
            0, mib=12,
        )

    far, far_other, next_other, prev_own = pick(
        ((2, False, 0), (2, True, 0), (1, True, 0), (3, False, 0))
    )
    far = y_shift(far, 1)
    far_other = y_shift(far_other, -1)
    below_cross = y_shift_cross(next_other, 1)
    above = y_shift(prev_own, -1)
    next_own, prev_other = pick(((1, False, YS - 1), (3, True, 1)), (far, far_other))
    below = y_shift(next_own, 1)
    above_cross = y_shift_cross(prev_other, -1)
    mine, mine_other = pick(((0, False, 0), (0, True, 0)))
    mine_cross = core_swap(mine_other)

    matmul = 2 * NB * NB * ROW * 3
    driving, last = call(
        forward_kernel, [SMEM] * 3 + [VMEM] * 15, [f32(4, NB, ROW), f32(NB, ROW)],
        (table, place, alive, mine, below, above, mine_cross, below_cross, above_cross,
         flux_jacobian, jacobian_came, *lift, *pivot, *l_split),
        26 * matmul,
        [pltpu.VMEM((NB, ROW), jnp.float32), pltpu.VMEM((2, 2, NB, ROW), jnp.float32)],
        mib=24,
    )
    driving, last, m1, m2, n1, n2 = lax.optimization_barrier((driving, last, m1, m2, n1, n2))
    split_scratch = [pltpu.VMEM((2, NB, NB), jnp.bfloat16)] * 4
    sweep, first = call(
        middle_kernel, [SMEM] + [VMEM] * 10, [f32(4, NB, ROW), f32(NB, ROW)],
        (alive, chip_shift(last, 1), chip_shift(last, 2), chip_shift(last, 3),
         m1, m2, driving, *l_split, *u_split), 18 * matmul, split_scratch, mib=24,
    )
    kept, sent = call(
        backward_kernel, [SMEM] * 2 + [VMEM] * 8, [f32(2, 2, NV, NB)] * 2,
        (core_ref, alive, chip_shift(first, -1), chip_shift(first, -2), chip_shift(first, -3),
         n1, n2, sweep, *u_split), 12 * matmul,
        [pltpu.VMEM((NB, ROW), jnp.float32)] + split_scratch,
    )
    came = core_swap(sent)
    return jnp.where(
        core == 0,
        jnp.concatenate([kept, came], axis=0),
        jnp.concatenate([came, kept], axis=0),
    )


def solution(mesh):
    return jax.shard_map(
        local,
        mesh=mesh,
        in_specs=(
            P("span", "line", None, None),
            P("span", "line", None, None),
            P("span", "line", None, None),
            P("span", "line", None, None),
            P("span", "line", None, None),
            P("span", "line", None, None),
            P(),
            P(),
            P("span"),
            P("span", None),
            P("span", None),
        ),
        out_specs=P("span", "line", None, None),
        check_vma=False,
    )
```

profile of v0, /device:TPU:1, one launch (start us, length us, event | category | flops | bytes accessed | tf_op | source)
XLA Modules:
  0.0 174.7 jit_solution(17574274541679000947)
XLA Ops:
  0.0 0.8 compare_convert_fusion
  0.9 1.3 broadcast_multiply_fusion
  2.1 0.8 fusion.1
  2.9 3.3 %collective-permute-start.2 = (f32[4,2,320,320]{3,2,1,0:T(8,128)}, f32[4,2,320,320]{3,2,1,0:T(8,128)}, u32[]{:S(2)}, u32[]{:S(2)}) collective-permute-start(f32[4,2,320,320]{3,2,1,0:T(8,128)} %kept), channel_id=1, source_target_pairs={{0,32},{32,0},{64,96},{96,64},{128,160},{160,128},{192,224},{224,1... | collective-permute-start | bytes 9830408 | tf_op jit(solution)/shard_map/ppermute | solution.py:50
  6.2 0.1 collective-permute-start.3
  6.3 0.4 collective-permute-start.7
  6.7 0.7 multiply_add_fusion
  7.5 1.0 collective-permute-start.4
  8.5 1.6 collective-permute-start
  10.1 0.7 dynamic_slice.3
  10.9 1.2 copy.14
  12.1 4.0 %collective-permute-start.1 = (f32[16,80,128]{2,1,0:T(8,128)S(1)}, f32[16,80,128]{2,1,0:T(8,128)S(1)}, u32[]{:S(2)}, u32[]{:S(2)}) collective-permute-start(f32[16,80,128]{2,1,0:T(8,128)S(1)} %bitcast.21), channel_id=1, source_target_pairs={{0,7},{1,0},{2,1},{3,2},{4,3},{5,4},{6,5},{7,6},{8,15},{9,8},{10,9... | collective-permute-start | bytes 1966088 | tf_op jit(solution)/shard_map/ppermute | solution.py:30
  16.1 0.7 compare_convert_fusion.1.alive
  16.8 0.9 fusion
  17.7 0.7 collective-permute-start.9
  18.3 7.3 %chain.2 = (bf16[2,4,320,320]{3,2,1,0:T(8,128)(2,1)}, bf16[2,4,320,320]{3,2,1,0:T(8,128)(2,1)}, f32[2,320,320]{2,1,0:T(8,128)}) custom-call(s32[1]{0:T(128)} %bitcast.core, f32[2,4]{1,0:T(2,128)} %compare_convert_fusion.1.alive, f32[4,2,320,320]{3,2,1,0:T(8,128)} %kept, f32[4,2,320,320]{3,2,1,0:T(8,128)} %collective-permute-done.2.came), custom_call_target="tpu_custom_call" | custom-call | flops 1179648000 | bytes 3276800 | tf_op jit(solution)/shard_map/chain/pallas_call | solution.py:345
  25.6 3.2 %collective-permute-done.up1 = f32[16,80,128]{2,1,0:T(8,128)S(1)} collective-permute-done((f32[16,80,128]{2,1,0:T(8,128)S(1)}, f32[16,80,128]{2,1,0:T(8,128)S(1)}, u32[]{:S(2)}, u32[]{:S(2)}) %collective-permute-start) | collective-permute-done | bytes 655392 | tf_op jit(solution)/shard_map/ppermute | solution.py:30
  28.8 1.0 collective-permute-start.8
  29.9 3.5 %collective-permute-start.6 = (f32[16,80,128]{2,1,0:T(8,128)S(1)}, f32[16,80,128]{2,1,0:T(8,128)S(1)}, u32[]{:S(2)}, u32[]{:S(2)}) collective-permute-start(f32[16,80,128]{2,1,0:T(8,128)S(1)} %collective-permute-done.1.down1), channel_id=1, source_target_pairs={{0,7},{1,0},{2,1},{3,2},{4,3},{5,4},{6,5},{7,6},{8,15},{9,8},{10,9... | collective-permute-start | bytes 1966088 | tf_op jit(solution)/shard_map/ppermute | solution.py:30
  33.3 7.2 %chain.3 = (bf16[2,4,320,320]{3,2,1,0:T(8,128)(2,1)}, bf16[2,4,320,320]{3,2,1,0:T(8,128)(2,1)}, f32[2,320,320]{2,1,0:T(8,128)}) custom-call(s32[1]{0:T(128)} %bitcast.core, f32[2,4]{1,0:T(2,128)} %compare_convert_fusion.1.alive, f32[4,2,320,320]{3,2,1,0:T(8,128)} %kept.1, f32[4,2,320,320]{3,2,1,0:T(8,128)} %collective-permute-done.3.came), custom_call_target="tpu_custom_call" | custom-call | flops 1179648000 | bytes 3276800 | tf_op jit(solution)/shard_map/chain/pallas_call | solution.py:345
  40.6 6.6 %collective-permute-done.5.up2 = f32[16,80,128]{2,1,0:T(8,128)} collective-permute-done((f32[16,80,128]{2,1,0:T(8,128)S(1)}, f32[16,80,128]{2,1,0:T(8,128)}, u32[]{:S(2)}, u32[]{:S(2)}) %collective-permute-start.5) | collective-permute-done | bytes 655392 | tf_op jit(solution)/shard_map/ppermute | solution.py:30
  47.2 0.9 copy-done.7
  48.1 1.2 collective-permute-start.10
  49.3 1.4 collective-permute-start.11
  50.8 3.9 %collective-permute-done.12 = s32[2,16]{1,0:T(2,128)S(1)} collective-permute-done((s32[2,16]{1,0:T(2,128)S(1)}, s32[2,16]{1,0:T(2,128)S(1)}, u32[]{:S(2)}, u32[]{:S(2)}) %collective-permute-start.12) | collective-permute-done | bytes 160 | tf_op jit(solution)/shard_map/ppermute | solution.py:35
  54.7 5.0 %own.1 = (bf16[2,4,320,320]{3,2,1,0:T(8,128)(2,1)}, bf16[2,4,320,320]{3,2,1,0:T(8,128)(2,1)}, f32[2,2,320,128]{3,2,1,0:T(8,128)}) custom-call(s32[1]{0:T(128)} %bitcast.core, f32[4,2,320,320]{3,2,1,0:T(8,128)} %kept.2, f32[4,2,320,320]{3,2,1,0:T(8,128)} %collective-permute-done.7.came, f32[4,2,64,320]{3,2,1,0:T(8,128)} %given_kept, ...), custom_call_target="tpu_custom_call" | custom-call | flops 314572800 | bytes 6553600 | tf_op jit(solution)/shard_map/own/pallas_call | solution.py:374
  59.7 4.3 %collective-permute-done.10.up.up3 = f32[16,80,128]{2,1,0:T(8,128)S(1)} collective-permute-done((f32[16,80,128]{2,1,0:T(8,128)}, f32[16,80,128]{2,1,0:T(8,128)S(1)}, u32[]{:S(2)}, u32[]{:S(2)}) %collective-permute-start.10) | collective-permute-done | bytes 655392 | tf_op jit(solution)/shard_map/ppermute | solution.py:30
  64.0 0.9 shard_map.109
  64.9 0.3 collective-permute-start.13
  65.2 2.4 %collective-permute-start.14 = (f32[8,80,128]{2,1,0:T(8,128)}, f32[8,80,128]{2,1,0:T(8,128)}, u32[]{:S(2)}, u32[]{:S(2)}) collective-permute-start(f32[8,80,128]{2,1,0:T(8,128)} %get-tuple-element.97), channel_id=1, source_target_pairs={{0,7},{1,0},{2,1},{3,2},{4,3},{5,4},{6,5},{7,6},{8,15},{9,8},{10,9... | collective-permute-start | bytes 983048 | tf_op jit(solution)/shard_map/ppermute | solution.py:30
  67.6 5.2 %collective-permute-done.13.up4 = f32[8,80,128]{2,1,0:T(8,128)S(1)} collective-permute-done((f32[8,80,128]{2,1,0:T(8,128)}, f32[8,80,128]{2,1,0:T(8,128)S(1)}, u32[]{:S(2)}, u32[]{:S(2)}) %collective-permute-start.13) | collective-permute-done | bytes 327712 | tf_op jit(solution)/shard_map/ppermute | solution.py:30
  72.9 1.1 copy-done.6
  74.0 1.1 copy-done.8
  75.1 2.4 %shard_map.111 = (f32[8,80,128]{2,1,0:T(8,128)S(1)}, f32[8,80,128]{2,1,0:T(8,128)S(1)}, f32[8,80,128]{2,1,0:T(8,128)S(1)}, f32[8,80,128]{2,1,0:T(8,128)S(1)}) custom-call(s32[4,16]{1,0:T(4,128)S(1)} %pad_add_fusion.table, s32[3]{0:T(128)S(1)} %pad_add_fusion.2.place, f32[16,80,128]{2,1,0:T(8,128)S(1)} %bitcast.22, ...), custom_call_target="tpu_custom_call" | custom-call | bytes 6553868 | tf_op jit(solution)/shard_map/pallas_call | solution.py:299
  77.6 2.7 %collective-permute-start.16 = (f32[8,80,128]{2,1,0:T(8,128)S(1)}, f32[8,80,128]{2,1,0:T(8,128)S(1)}, u32[]{:S(2)}, u32[]{:S(2)}) collective-permute-start(f32[8,80,128]{2,1,0:T(8,128)S(1)} %get-tuple-element.100), channel_id=1, source_target_pairs={{0,24},{1,25},{2,26},{3,27},{4,28},{5,29},{6,30},{7,31},{8,0},{9,1... | collective-permute-start | bytes 983048 | tf_op jit(solution)/shard_map/ppermute | solution.py:35
  80.3 5.9 %collective-permute-start.20 = (f32[8,80,128]{2,1,0:T(8,128)S(1)}, f32[8,80,128]{2,1,0:T(8,128)S(1)}, u32[]{:S(2)}, u32[]{:S(2)}) collective-permute-start(f32[8,80,128]{2,1,0:T(8,128)S(1)} %get-tuple-element.104), channel_id=1, source_target_pairs={{0,40},{1,41},{2,42},{3,43},{4,44},{5,45},{6,46},{7,47},{8,48},{9,... | collective-permute-start | bytes 983048 | tf_op jit(solution)/shard_map/ppermute | solution.py:46
  86.2 2.0 %shard_map.110 = (f32[8,80,128]{2,1,0:T(8,128)S(1)}, f32[8,80,128]{2,1,0:T(8,128)S(1)}) custom-call(s32[4,16]{1,0:T(4,128)S(1)} %pad_add_fusion.table, s32[3]{0:T(128)S(1)} %pad_add_fusion.2.place, f32[16,80,128]{2,1,0:T(8,128)S(1)} %bitcast.23, f32[16,80,128]{2,1,0:T(8,128)S(1)} %collective-permute-done.up1, f32[16,80,128]{2,1,0:T(8,128)} %collective-permute-done.5.up2, ...), custom_call_target="tpu_custom_call" | custom-call | bytes 5898508 | tf_op jit(solution)/shard_map/pallas_call | solution.py:299
  88.3 0.1 collective-permute-start.19
  88.4 2.2 %shard_map.112 = (f32[8,80,128]{2,1,0:T(8,128)S(1)}, f32[8,80,128]{2,1,0:T(8,128)S(1)}) custom-call(s32[4,16]{1,0:T(4,128)S(1)} %pad_add_fusion.table, s32[3]{0:T(128)S(1)} %pad_add_fusion.2.place, f32[16,80,128]{2,1,0:T(8,128)S(1)} %bitcast.24, f32[16,80,128]{2,1,0:T(8,128)S(1)} %collective-permute-done.up1, f32[16,80,128]{2,1,0:T(8,128)} %collective-permute-done.5.up2, ...), custom_call_target="tpu_custom_call" | custom-call | bytes 6553868 | tf_op jit(solution)/shard_map/pallas_call | solution.py:299
  90.6 1.3 collective-permute-start.24
  92.0 1.3 collective-permute-start.25
  93.3 3.5 %collective-permute-done.20.below_cross = f32[8,80,128]{2,1,0:T(8,128)S(1)} collective-permute-done((f32[8,80,128]{2,1,0:T(8,128)S(1)}, f32[8,80,128]{2,1,0:T(8,128)S(1)}, u32[]{:S(2)}, u32[]{:S(2)}) %collective-permute-start.20) | collective-permute-done | bytes 327712 | tf_op jit(solution)/shard_map/ppermute | solution.py:46
  96.8 0.7 collective-permute-start.22
  97.5 0.7 collective-permute-start.23
  98.2 2.6 %collective-permute-done.17.below = f32[8,80,128]{2,1,0:T(8,128)S(1)} collective-permute-done((f32[8,80,128]{2,1,0:T(8,128)S(1)}, f32[8,80,128]{2,1,0:T(8,128)S(1)}, u32[]{:S(2)}, u32[]{:S(2)}) %collective-permute-start.17) | collective-permute-done | bytes 327712 | tf_op jit(solution)/shard_map/ppermute | solution.py:35
  100.8 3.4 %collective-permute-start.21 = (f32[8,80,128]{2,1,0:T(8,128)S(1)}, f32[8,80,128]{2,1,0:T(8,128)S(1)}, u32[]{:S(2)}, u32[]{:S(2)}) collective-permute-start(f32[8,80,128]{2,1,0:T(8,128)S(1)} %get-tuple-element.105), channel_id=1, source_target_pairs={{0,56},{1,57},{2,58},{3,59},{4,60},{5,61},{6,62},{7,63},{8,32},{9,... | collective-permute-start | bytes 983048 | tf_op jit(solution)/shard_map/ppermute | solution.py:46
  104.2 7.2 %collective-permute-done.21.above_cross = f32[8,80,128]{2,1,0:T(8,128)S(1)} collective-permute-done((f32[8,80,128]{2,1,0:T(8,128)S(1)}, f32[8,80,128]{2,1,0:T(8,128)S(1)}, u32[]{:S(2)}, u32[]{:S(2)}) %collective-permute-start.21) | collective-permute-done | bytes 327712 | tf_op jit(solution)/shard_map/ppermute | solution.py:46
  111.5 7.6 %shard_map.113 = (f32[4,320,128]{2,1,0:T(8,128)S(1)}, f32[320,128]{1,0:T(8,128)S(1)}) custom-call(s32[4,16]{1,0:T(4,128)S(1)} %pad_add_fusion.table, s32[3]{0:T(128)S(1)} %pad_add_fusion.2.place, f32[2,4]{1,0:T(2,128)S(1)} %copy-done.16, f32[8,80,128]{2,1,0:T(8,128)S(1)} %get-tuple-element.98.mine, f32[8,80,128]{2,1,0:T(8,128)S(1)} %collective-permute-done.17.below, ...), custom_call_target="tpu_custom_call" | custom-call | flops 2044723200 | bytes 19005740 | tf_op jit(solution)/shard_map/pallas_call | solution.py:299
  119.1 15.9 %collective-permute-start.26 = (f32[320,128]{1,0:T(8,128)S(1)}, f32[320,128]{1,0:T(8,128)S(1)}, u32[]{:S(2)}, u32[]{:S(2)}) collective-permute-start(f32[320,128]{1,0:T(8,128)S(1)} %get-tuple-element.117), channel_id=1, source_target_pairs={{0,64},{32,96},{64,128},{96,160},{128,192},{160,224},{1,65},{33,97... | collective-permute-start | bytes 491528 | tf_op jit(solution)/shard_map/ppermute | solution.py:60
  135.0 6.9 %collective-permute-start.27 = (f32[320,128]{1,0:T(8,128)S(1)}, f32[320,128]{1,0:T(8,128)S(1)}, u32[]{:S(2)}, u32[]{:S(2)}) collective-permute-start(f32[320,128]{1,0:T(8,128)S(1)} %get-tuple-element.117), channel_id=1, source_target_pairs={{0,128},{32,160},{64,192},{96,224},{1,129},{33,161},{65,193},{97,2... | collective-permute-start | bytes 491528 | tf_op jit(solution)/shard_map/ppermute | solution.py:60
  142.0 1.3 collective-permute-start.28
  143.3 1.0 collective-permute-done.27.mid
  144.2 1.3 collective-permute-done.28.far
  145.5 4.7 %shard_map.114 = (f32[4,320,128]{2,1,0:T(8,128)S(1)}, f32[320,128]{1,0:T(8,128)S(1)}) custom-call(f32[2,4]{1,0:T(2,128)S(1)} %copy-done.16, f32[320,128]{1,0:T(8,128)S(1)} %collective-permute-done.26.near, f32[320,128]{1,0:T(8,128)S(1)} %collective-permute-done.27.mid, f32[320,128]{1,0:T(8,128)S(1)} %collective-permute-done.28.far, ...), custom_call_target="tpu_custom_call" | custom-call | flops 1415577600 | bytes 16711712 | tf_op jit(solution)/shard_map/pallas_call | solution.py:299
  150.2 1.3 collective-permute-start.29
  151.5 1.3 collective-permute-start.30
  152.8 1.3 collective-permute-start.31
  154.1 2.2 %collective-permute-done.29.near = f32[320,128]{1,0:T(8,128)S(1)} collective-permute-done((f32[320,128]{1,0:T(8,128)S(1)}, f32[320,128]{1,0:T(8,128)S(1)}, u32[]{:S(2)}, u32[]{:S(2)}) %collective-permute-start.29) | collective-permute-done | bytes 163872 | tf_op jit(solution)/shard_map/ppermute | solution.py:60
  156.3 2.8 %collective-permute-done.30.mid = f32[320,128]{1,0:T(8,128)S(1)} collective-permute-done((f32[320,128]{1,0:T(8,128)S(1)}, f32[320,128]{1,0:T(8,128)S(1)}, u32[]{:S(2)}, u32[]{:S(2)}) %collective-permute-start.30) | collective-permute-done | bytes 163872 | tf_op jit(solution)/shard_map/ppermute | solution.py:60
  159.1 2.8 %collective-permute-done.31.far = f32[320,128]{1,0:T(8,128)S(1)} collective-permute-done((f32[320,128]{1,0:T(8,128)S(1)}, f32[320,128]{1,0:T(8,128)S(1)}, u32[]{:S(2)}, u32[]{:S(2)}) %collective-permute-start.31) | collective-permute-done | bytes 163872 | tf_op jit(solution)/shard_map/ppermute | solution.py:60
  161.9 3.8 %shard_map.115 = (f32[2,2,64,320]{3,2,1,0:T(8,128)S(1)}, f32[2,2,64,320]{3,2,1,0:T(8,128)S(1)}) custom-call(s32[1]{0:T(128)} %bitcast.core, f32[2,4]{1,0:T(2,128)S(1)} %copy-done.16, f32[320,128]{1,0:T(8,128)S(1)} %collective-permute-done.29.near, f32[320,128]{1,0:T(8,128)S(1)} %collective-permute-done.30.mid, f32[320,128]{1,0:T(8,128)S(1)} %collective-permute-done.31.far, ...), custom_call_target="tpu_custom_call" | custom-call | flops 943718400 | bytes 9994276 | tf_op jit(solution)/shard_map/pallas_call | solution.py:299
  165.7 6.7 %collective-permute-start.32 = (f32[2,2,64,320]{3,2,1,0:T(8,128)S(1)}, f32[2,2,64,320]{3,2,1,0:T(8,128)S(1)}, u32[]{:S(2)}, u32[]{:S(2)}) collective-permute-start(f32[2,2,64,320]{3,2,1,0:T(8,128)S(1)} %get-tuple-element.128), channel_id=1, source_target_pairs={{0,32},{32,0},{64,96},{96,64},{128,160},{160,128},{192,224},{224,1... | collective-permute-start | bytes 983048 | tf_op jit(solution)/shard_map/ppermute | solution.py:50
  172.4 1.3 collective-permute-done.32
  173.7 0.9 maximum_select_fusion
  (65 shorter events, 0.6 us)
Async XLA Ops:
  0.0 2.1 %copy-start = (f32[320,320]{1,0:T(8,128)S(1)}, f32[320,320]{1,0:T(8,128)}, u32[]{:S(2)}) copy-start(f32[320,320]{1,0:T(8,128)} %param.17) | copy-start | bytes 1228804
  0.0 17.7 %copy-start.11 = (f32[4,2,80,320]{3,2,1,0:T(8,128)S(1)}, f32[4,2,80,320]{3,2,1,0:T(8,128)}, u32[]{:S(2)}) copy-start(f32[4,2,80,320]{3,2,1,0:T(8,128)} %jacobian) | copy-start | bytes 2457604
  2.9 14.8 %collective-permute-start.2 = (f32[4,2,320,320]{3,2,1,0:T(8,128)}, f32[4,2,320,320]{3,2,1,0:T(8,128)}, u32[]{:S(2)}, u32[]{:S(2)}) collective-permute-start(f32[4,2,320,320]{3,2,1,0:T(8,128)} %kept), channel_id=1, source_target_pairs={{0,32},{32,0},{64,96},{96,64},{128,160},{160,128},{192,224},{224,1... | collective-permute-start | bytes 9830408 | tf_op jit(solution)/shard_map/ppermute | solution.py:50
  6.2 23.7 %collective-permute-start.3 = (f32[4,2,320,320]{3,2,1,0:T(8,128)}, f32[4,2,320,320]{3,2,1,0:T(8,128)}, u32[]{:S(2)}, u32[]{:S(2)}) collective-permute-start(f32[4,2,320,320]{3,2,1,0:T(8,128)} %kept.1), channel_id=1, source_target_pairs={{0,32},{32,0},{64,96},{96,64},{128,160},{160,128},{192,224},{224,1... | collective-permute-start | bytes 9830408 | tf_op jit(solution)/shard_map/ppermute | solution.py:50
  6.3 34.3 %collective-permute-start.7 = (f32[4,2,320,320]{3,2,1,0:T(8,128)}, f32[4,2,320,320]{3,2,1,0:T(8,128)}, u32[]{:S(2)}, u32[]{:S(2)}) collective-permute-start(f32[4,2,320,320]{3,2,1,0:T(8,128)} %kept.2), channel_id=1, source_target_pairs={{0,32},{32,0},{64,96},{96,64},{128,160},{160,128},{192,224},{224,1... | collective-permute-start | bytes 9830408 | tf_op jit(solution)/shard_map/ppermute | solution.py:50
  7.5 4.6 %collective-permute-start.4 = (s32[1,16]{1,0:T(1,128)S(1)}, s32[1,16]{1,0:T(1,128)S(1)}, u32[]{:S(2)}, u32[]{:S(2)}) collective-permute-start(s32[1,16]{1,0:T(1,128)S(1)} %reshape.73), channel_id=1, source_target_pairs={{0,24},{1,25},{2,26},{3,27},{4,28},{5,29},{6,30},{7,31},{8,0},{9,1... | collective-permute-start | bytes 200 | tf_op jit(solution)/shard_map/ppermute | solution.py:35
  8.5 20.3 %collective-permute-start = (f32[16,80,128]{2,1,0:T(8,128)S(1)}, f32[16,80,128]{2,1,0:T(8,128)S(1)}, u32[]{:S(2)}, u32[]{:S(2)}) collective-permute-start(f32[16,80,128]{2,1,0:T(8,128)S(1)} %bitcast.20), channel_id=1, source_target_pairs={{0,1},{1,2},{2,3},{3,4},{4,5},{5,6},{6,7},{7,0},{8,9},{9,10},{10,1... | collective-permute-start | bytes 1966088 | tf_op jit(solution)/shard_map/ppermute | solution.py:30
  12.1 17.7 %collective-permute-start.1 = (f32[16,80,128]{2,1,0:T(8,128)S(1)}, f32[16,80,128]{2,1,0:T(8,128)S(1)}, u32[]{:S(2)}, u32[]{:S(2)}) collective-permute-start(f32[16,80,128]{2,1,0:T(8,128)S(1)} %bitcast.21), channel_id=1, source_target_pairs={{0,7},{1,0},{2,1},{3,2},{4,3},{5,4},{6,5},{7,6},{8,15},{9,8},{10,9... | collective-permute-start | bytes 1966088 | tf_op jit(solution)/shard_map/ppermute | solution.py:30
  17.7 22.9 %collective-permute-start.9 = (f32[4,2,80,320]{3,2,1,0:T(8,128)S(1)}, f32[4,2,80,320]{3,2,1,0:T(8,128)}, u32[]{:S(2)}, u32[]{:S(2)}) collective-permute-start(f32[4,2,80,320]{3,2,1,0:T(8,128)S(1)} %copy-done.11), channel_id=1, source_target_pairs={{0,32},{32,0},{64,96},{96,64},{128,160},{160,128},{192,224},{224,1... | collective-permute-start | bytes 2457608 | tf_op jit(solution)/shard_map/ppermute | solution.py:50
  28.8 11.8 %collective-permute-start.8 = (f32[4,2,64,320]{3,2,1,0:T(8,128)}, f32[4,2,64,320]{3,2,1,0:T(8,128)}, u32[]{:S(2)}, u32[]{:S(2)}) collective-permute-start(f32[4,2,64,320]{3,2,1,0:T(8,128)} %given_kept), channel_id=1, source_target_pairs={{0,32},{32,0},{64,96},{96,64},{128,160},{160,128},{192,224},{224,1... | collective-permute-start | bytes 1966088 | tf_op jit(solution)/shard_map/ppermute | solution.py:50
  29.8 10.8 %copy-start.5 = (f32[16,80,128]{2,1,0:T(8,128)}, f32[16,80,128]{2,1,0:T(8,128)S(1)}, u32[]{:S(2)}) copy-start(f32[16,80,128]{2,1,0:T(8,128)S(1)} %collective-permute-done.1.down1) | copy-start | bytes 1966084
  29.8 17.4 %collective-permute-start.5 = (f32[16,80,128]{2,1,0:T(8,128)S(1)}, f32[16,80,128]{2,1,0:T(8,128)}, u32[]{:S(2)}, u32[]{:S(2)}) collective-permute-start(f32[16,80,128]{2,1,0:T(8,128)S(1)} %collective-permute-done.up1), channel_id=1, source_target_pairs={{0,1},{1,2},{2,3},{3,4},{4,5},{5,6},{6,7},{7,0},{8,9},{9,10},{10,1... | collective-permute-start | bytes 1966088 | tf_op jit(solution)/shard_map/ppermute | solution.py:30
  29.9 17.4 %collective-permute-start.6 = (f32[16,80,128]{2,1,0:T(8,128)S(1)}, f32[16,80,128]{2,1,0:T(8,128)S(1)}, u32[]{:S(2)}, u32[]{:S(2)}) collective-permute-start(f32[16,80,128]{2,1,0:T(8,128)S(1)} %collective-permute-done.1.down1), channel_id=1, source_target_pairs={{0,7},{1,0},{2,1},{3,2},{4,3},{5,4},{6,5},{7,6},{8,15},{9,8},{10,9... | collective-permute-start | bytes 1966088 | tf_op jit(solution)/shard_map/ppermute | solution.py:30
  47.2 0.9 copy-start.7
  48.1 15.9 %collective-permute-start.10 = (f32[16,80,128]{2,1,0:T(8,128)}, f32[16,80,128]{2,1,0:T(8,128)S(1)}, u32[]{:S(2)}, u32[]{:S(2)}) collective-permute-start(f32[16,80,128]{2,1,0:T(8,128)} %collective-permute-done.5.up2), channel_id=1, source_target_pairs={{0,1},{1,2},{2,3},{3,4},{4,5},{5,6},{6,7},{7,0},{8,9},{9,10},{10,1... | collective-permute-start | bytes 1966088 | tf_op jit(solution)/shard_map/ppermute | solution.py:30
  49.3 14.7 %collective-permute-start.11 = (f32[16,80,128]{2,1,0:T(8,128)}, f32[16,80,128]{2,1,0:T(8,128)S(1)}, u32[]{:S(2)}, u32[]{:S(2)}) collective-permute-start(f32[16,80,128]{2,1,0:T(8,128)} %copy-done.7), channel_id=1, source_target_pairs={{0,7},{1,0},{2,1},{3,2},{4,3},{5,4},{6,5},{7,6},{8,15},{9,8},{10,9... | collective-permute-start | bytes 1966088 | tf_op jit(solution)/shard_map/ppermute | solution.py:30
  50.8 3.9 %collective-permute-start.12 = (s32[2,16]{1,0:T(2,128)S(1)}, s32[2,16]{1,0:T(2,128)S(1)}, u32[]{:S(2)}, u32[]{:S(2)}) collective-permute-start(s32[2,16]{1,0:T(2,128)S(1)} %pad_add_fusion.1), channel_id=1, source_target_pairs={{0,16},{1,17},{2,18},{3,19},{4,20},{5,21},{6,22},{7,23},{8,24},{9,... | collective-permute-start | bytes 392 | tf_op jit(solution)/shard_map/ppermute | solution.py:35
  64.9 8.0 %collective-permute-start.13 = (f32[8,80,128]{2,1,0:T(8,128)}, f32[8,80,128]{2,1,0:T(8,128)S(1)}, u32[]{:S(2)}, u32[]{:S(2)}) collective-permute-start(f32[8,80,128]{2,1,0:T(8,128)} %get-tuple-element.96), channel_id=1, source_target_pairs={{0,1},{1,2},{2,3},{3,4},{4,5},{5,6},{6,7},{7,0},{8,9},{9,10},{10,1... | collective-permute-start | bytes 983048 | tf_op jit(solution)/shard_map/ppermute | solution.py:30
  65.2 7.7 %collective-permute-start.14 = (f32[8,80,128]{2,1,0:T(8,128)}, f32[8,80,128]{2,1,0:T(8,128)}, u32[]{:S(2)}, u32[]{:S(2)}) collective-permute-start(f32[8,80,128]{2,1,0:T(8,128)} %get-tuple-element.97), channel_id=1, source_target_pairs={{0,7},{1,0},{2,1},{3,2},{4,3},{5,4},{6,5},{7,6},{8,15},{9,8},{10,9... | collective-permute-start | bytes 983048 | tf_op jit(solution)/shard_map/ppermute | solution.py:30
  72.9 1.1 copy-start.6
  74.0 1.1 copy-start.8
  75.1 15.6 %copy-start.18 = (f32[2,320,320]{2,1,0:T(8,128)S(1)}, f32[2,320,320]{2,1,0:T(8,128)}, u32[]{:S(2)}) copy-start(f32[2,320,320]{2,1,0:T(8,128)} %get-tuple-element.81) | copy-start | bytes 2457604
  77.5 10.8 %collective-permute-start.15 = (f32[8,80,128]{2,1,0:T(8,128)S(1)}, f32[8,80,128]{2,1,0:T(8,128)S(1)}, u32[]{:S(2)}, u32[]{:S(2)}) collective-permute-start(f32[8,80,128]{2,1,0:T(8,128)S(1)} %get-tuple-element.99), channel_id=1, source_target_pairs={{0,8},{1,9},{2,10},{3,11},{4,12},{5,13},{6,14},{7,15},{8,16},{9,17... | collective-permute-start | bytes 983048 | tf_op jit(solution)/shard_map/ppermute | solution.py:35
  77.6 10.8 %collective-permute-start.16 = (f32[8,80,128]{2,1,0:T(8,128)S(1)}, f32[8,80,128]{2,1,0:T(8,128)S(1)}, u32[]{:S(2)}, u32[]{:S(2)}) collective-permute-start(f32[8,80,128]{2,1,0:T(8,128)S(1)} %get-tuple-element.100), channel_id=1, source_target_pairs={{0,24},{1,25},{2,26},{3,27},{4,28},{5,29},{6,30},{7,31},{8,0},{9,1... | collective-permute-start | bytes 983048 | tf_op jit(solution)/shard_map/ppermute | solution.py:35
  80.3 11.7 %collective-permute-start.18 = (f32[8,80,128]{2,1,0:T(8,128)S(1)}, f32[8,80,128]{2,1,0:T(8,128)S(1)}, u32[]{:S(2)}, u32[]{:S(2)}) collective-permute-start(f32[8,80,128]{2,1,0:T(8,128)S(1)} %get-tuple-element.102), channel_id=1, source_target_pairs={{0,24},{1,25},{2,26},{3,27},{4,28},{5,29},{6,30},{7,31},{8,0},{9,1... | collective-permute-start | bytes 983048 | tf_op jit(solution)/shard_map/ppermute | solution.py:35
  80.3 16.5 %collective-permute-start.20 = (f32[8,80,128]{2,1,0:T(8,128)S(1)}, f32[8,80,128]{2,1,0:T(8,128)S(1)}, u32[]{:S(2)}, u32[]{:S(2)}) collective-permute-start(f32[8,80,128]{2,1,0:T(8,128)S(1)} %get-tuple-element.104), channel_id=1, source_target_pairs={{0,40},{1,41},{2,42},{3,43},{4,44},{5,45},{6,46},{7,47},{8,48},{9,... | collective-permute-start | bytes 983048 | tf_op jit(solution)/shard_map/ppermute | solution.py:46
  86.2 10.6 %copy-start.17 = (f32[2,320,320]{2,1,0:T(8,128)S(1)}, f32[2,320,320]{2,1,0:T(8,128)}, u32[]{:S(2)}) copy-start(f32[2,320,320]{2,1,0:T(8,128)} %get-tuple-element.116) | copy-start | bytes 2457604
  86.2 25.2 %copy-start.10 = (bf16[2,4,320,320]{3,2,1,0:T(8,128)(2,1)S(1)}, bf16[2,4,320,320]{3,2,1,0:T(8,128)(2,1)}, u32[]{:S(2)}) copy-start(bf16[2,4,320,320]{3,2,1,0:T(8,128)(2,1)} %get-tuple-element.91) | copy-start | bytes 4915204
  86.2 25.2 %copy-start.12 = (f32[4,2,80,320]{3,2,1,0:T(8,128)S(1)}, f32[4,2,80,320]{3,2,1,0:T(8,128)}, u32[]{:S(2)}) copy-start(f32[4,2,80,320]{3,2,1,0:T(8,128)} %jacobian) | copy-start | bytes 2457604
  86.2 25.2 %copy-start.13 = (bf16[320,320]{1,0:T(8,128)(2,1)S(1)}, bf16[320,320]{1,0:T(8,128)(2,1)}, u32[]{:S(2)}) copy-start(bf16[320,320]{1,0:T(8,128)(2,1)} %get-tuple-element.108.lift_low) | copy-start | bytes 614404
  86.2 25.2 %copy-start.14 = (bf16[320,320]{1,0:T(8,128)(2,1)S(1)}, bf16[320,320]{1,0:T(8,128)(2,1)}, u32[]{:S(2)}) copy-start(bf16[320,320]{1,0:T(8,128)(2,1)} %get-tuple-element.107.lift_high) | copy-start | bytes 614404
  86.2 25.2 %copy-start.15 = (f32[2,2,320,128]{3,2,1,0:T(8,128)S(1)}, f32[2,2,320,128]{3,2,1,0:T(8,128)}, u32[]{:S(2)}) copy-start(f32[2,2,320,128]{3,2,1,0:T(8,128)} %get-tuple-element.111.own) | copy-start | bytes 1966084
  88.2 23.2 %copy-start.1 = (bf16[2,4,320,320]{3,2,1,0:T(8,128)(2,1)S(1)}, bf16[2,4,320,320]{3,2,1,0:T(8,128)(2,1)}, u32[]{:S(2)}) copy-start(bf16[2,4,320,320]{3,2,1,0:T(8,128)(2,1)} %get-tuple-element.69) | copy-start | bytes 4915204
  88.2 23.2 %copy-start.2 = (bf16[2,4,320,320]{3,2,1,0:T(8,128)(2,1)S(1)}, bf16[2,4,320,320]{3,2,1,0:T(8,128)(2,1)}, u32[]{:S(2)}) copy-start(bf16[2,4,320,320]{3,2,1,0:T(8,128)(2,1)} %get-tuple-element.70) | copy-start | bytes 4915204
  88.2 23.2 %copy-start.9 = (bf16[2,4,320,320]{3,2,1,0:T(8,128)(2,1)S(1)}, bf16[2,4,320,320]{3,2,1,0:T(8,128)(2,1)}, u32[]{:S(2)}) copy-start(bf16[2,4,320,320]{3,2,1,0:T(8,128)(2,1)} %get-tuple-element.90) | copy-start | bytes 4915204
  88.2 23.2 %copy-start.16 = (f32[2,4]{1,0:T(2,128)S(1)}, f32[2,4]{1,0:T(2,128)}, u32[]{:S(2)}) copy-start(f32[2,4]{1,0:T(2,128)} %compare_convert_fusion.1.alive) | copy-start | bytes 100
  88.3 9.3 %collective-permute-start.19 = (f32[8,80,128]{2,1,0:T(8,128)S(1)}, f32[8,80,128]{2,1,0:T(8,128)S(1)}, u32[]{:S(2)}, u32[]{:S(2)}) collective-permute-start(f32[8,80,128]{2,1,0:T(8,128)S(1)} %get-tuple-element.103), channel_id=1, source_target_pairs={{0,32},{32,0},{64,96},{96,64},{128,160},{160,128},{192,224},{224,1... | collective-permute-start | bytes 983048 | tf_op jit(solution)/shard_map/ppermute | solution.py:50
  90.5 10.3 %collective-permute-start.17 = (f32[8,80,128]{2,1,0:T(8,128)S(1)}, f32[8,80,128]{2,1,0:T(8,128)S(1)}, u32[]{:S(2)}, u32[]{:S(2)}) collective-permute-start(f32[8,80,128]{2,1,0:T(8,128)S(1)} %get-tuple-element.101), channel_id=1, source_target_pairs={{0,8},{1,9},{2,10},{3,11},{4,12},{5,13},{6,14},{7,15},{8,16},{9,17... | collective-permute-start | bytes 983048 | tf_op jit(solution)/shard_map/ppermute | solution.py:35
  90.6 28.4 %collective-permute-start.24 = (f32[2,320,320]{2,1,0:T(8,128)S(1)}, f32[2,320,320]{2,1,0:T(8,128)S(1)}, u32[]{:S(2)}, u32[]{:S(2)}) collective-permute-start(f32[2,320,320]{2,1,0:T(8,128)S(1)} %copy-done.18), channel_id=1, source_target_pairs={{128,64},{160,96},{64,0},{96,32},{129,65},{161,97},{65,1},{97,33},... | collective-permute-start | bytes 2457608 | tf_op jit(solution)/shard_map/ppermute | solution.py:60
  92.0 27.1 %collective-permute-start.25 = (f32[2,320,320]{2,1,0:T(8,128)S(1)}, f32[2,320,320]{2,1,0:T(8,128)S(1)}, u32[]{:S(2)}, u32[]{:S(2)}) collective-permute-start(f32[2,320,320]{2,1,0:T(8,128)S(1)} %copy-done.18), channel_id=1, source_target_pairs={{128,0},{160,32},{129,1},{161,33},{130,2},{162,34},{131,3},{163,35... | collective-permute-start | bytes 2457608 | tf_op jit(solution)/shard_map/ppermute | solution.py:60
  96.8 22.3 %collective-permute-start.22 = (f32[2,320,320]{2,1,0:T(8,128)S(1)}, f32[2,320,320]{2,1,0:T(8,128)S(1)}, u32[]{:S(2)}, u32[]{:S(2)}) collective-permute-start(f32[2,320,320]{2,1,0:T(8,128)S(1)} %copy-done.17), channel_id=1, source_target_pairs={{64,128},{96,160},{128,192},{160,224},{65,129},{97,161},{129,193},... | collective-permute-start | bytes 2457608 | tf_op jit(solution)/shard_map/ppermute | solution.py:60
  97.5 21.6 %collective-permute-start.23 = (f32[2,320,320]{2,1,0:T(8,128)S(1)}, f32[2,320,320]{2,1,0:T(8,128)S(1)}, u32[]{:S(2)}, u32[]{:S(2)}) collective-permute-start(f32[2,320,320]{2,1,0:T(8,128)S(1)} %copy-done.17), channel_id=1, source_target_pairs={{64,192},{96,224},{65,193},{97,225},{66,194},{98,226},{67,195},{99... | collective-permute-start | bytes 2457608 | tf_op jit(solution)/shard_map/ppermute | solution.py:60
  100.8 10.5 %collective-permute-start.21 = (f32[8,80,128]{2,1,0:T(8,128)S(1)}, f32[8,80,128]{2,1,0:T(8,128)S(1)}, u32[]{:S(2)}, u32[]{:S(2)}) collective-permute-start(f32[8,80,128]{2,1,0:T(8,128)S(1)} %get-tuple-element.105), channel_id=1, source_target_pairs={{0,56},{1,57},{2,58},{3,59},{4,60},{5,61},{6,62},{7,63},{8,32},{9,... | collective-permute-start | bytes 983048 | tf_op jit(solution)/shard_map/ppermute | solution.py:46
  111.4 34.1 %copy-start.3 = (bf16[2,4,320,320]{3,2,1,0:T(8,128)(2,1)S(1)}, bf16[2,4,320,320]{3,2,1,0:T(8,128)(2,1)}, u32[]{:S(2)}) copy-start(bf16[2,4,320,320]{3,2,1,0:T(8,128)(2,1)} %get-tuple-element.79) | copy-start | bytes 4915204
  111.5 34.0 %copy-start.4 = (bf16[2,4,320,320]{3,2,1,0:T(8,128)(2,1)S(1)}, bf16[2,4,320,320]{3,2,1,0:T(8,128)(2,1)}, u32[]{:S(2)}) copy-start(bf16[2,4,320,320]{3,2,1,0:T(8,128)(2,1)} %get-tuple-element.80) | copy-start | bytes 4915204
  119.1 24.2 %collective-permute-start.26 = (f32[320,128]{1,0:T(8,128)S(1)}, f32[320,128]{1,0:T(8,128)S(1)}, u32[]{:S(2)}, u32[]{:S(2)}) collective-permute-start(f32[320,128]{1,0:T(8,128)S(1)} %get-tuple-element.117), channel_id=1, source_target_pairs={{0,64},{32,96},{64,128},{96,160},{128,192},{160,224},{1,65},{33,97... | collective-permute-start | bytes 491528 | tf_op jit(solution)/shard_map/ppermute | solution.py:60
  135.0 9.2 %collective-permute-start.27 = (f32[320,128]{1,0:T(8,128)S(1)}, f32[320,128]{1,0:T(8,128)S(1)}, u32[]{:S(2)}, u32[]{:S(2)}) collective-permute-start(f32[320,128]{1,0:T(8,128)S(1)} %get-tuple-element.117), channel_id=1, source_target_pairs={{0,128},{32,160},{64,192},{96,224},{1,129},{33,161},{65,193},{97,2... | collective-permute-start | bytes 491528 | tf_op jit(solution)/shard_map/ppermute | solution.py:60
  142.0 3.5 %collective-permute-start.28 = (f32[320,128]{1,0:T(8,128)S(1)}, f32[320,128]{1,0:T(8,128)S(1)}, u32[]{:S(2)}, u32[]{:S(2)}) collective-permute-start(f32[320,128]{1,0:T(8,128)S(1)} %get-tuple-element.117), channel_id=1, source_target_pairs={{0,192},{32,224},{1,193},{33,225},{2,194},{34,226},{3,195},{35,227... | collective-permute-start | bytes 491528 | tf_op jit(solution)/shard_map/ppermute | solution.py:60
  150.2 6.1 %collective-permute-start.29 = (f32[320,128]{1,0:T(8,128)S(1)}, f32[320,128]{1,0:T(8,128)S(1)}, u32[]{:S(2)}, u32[]{:S(2)}) collective-permute-start(f32[320,128]{1,0:T(8,128)S(1)} %get-tuple-element.123), channel_id=1, source_target_pairs={{64,0},{96,32},{128,64},{160,96},{192,128},{224,160},{65,1},{97,33... | collective-permute-start | bytes 491528 | tf_op jit(solution)/shard_map/ppermute | solution.py:60
  151.5 7.6 %collective-permute-start.30 = (f32[320,128]{1,0:T(8,128)S(1)}, f32[320,128]{1,0:T(8,128)S(1)}, u32[]{:S(2)}, u32[]{:S(2)}) collective-permute-start(f32[320,128]{1,0:T(8,128)S(1)} %get-tuple-element.123), channel_id=1, source_target_pairs={{128,0},{160,32},{192,64},{224,96},{129,1},{161,33},{193,65},{225,... | collective-permute-start | bytes 491528 | tf_op jit(solution)/shard_map/ppermute | solution.py:60
  152.8 9.1 %collective-permute-start.31 = (f32[320,128]{1,0:T(8,128)S(1)}, f32[320,128]{1,0:T(8,128)S(1)}, u32[]{:S(2)}, u32[]{:S(2)}) collective-permute-start(f32[320,128]{1,0:T(8,128)S(1)} %get-tuple-element.123), channel_id=1, source_target_pairs={{192,0},{224,32},{193,1},{225,33},{194,2},{226,34},{195,3},{227,35... | collective-permute-start | bytes 491528 | tf_op jit(solution)/shard_map/ppermute | solution.py:60
  165.7 8.0 %collective-permute-start.32 = (f32[2,2,64,320]{3,2,1,0:T(8,128)S(1)}, f32[2,2,64,320]{3,2,1,0:T(8,128)S(1)}, u32[]{:S(2)}, u32[]{:S(2)}) collective-permute-start(f32[2,2,64,320]{3,2,1,0:T(8,128)S(1)} %get-tuple-element.128), channel_id=1, source_target_pairs={{0,32},{32,0},{64,96},{96,64},{128,160},{160,128},{192,224},{224,1... | collective-permute-start | bytes 983048 | tf_op jit(solution)/shard_map/ppermute | solution.py:50
where the time goes:
time: 175 us
  starting transfers between devices  71.9 us (41%)
  waiting for transfers between devices  48 us (27%)
  Pallas kernels  43.1 us (25%)
  other arithmetic  5.35 us (3%)
  local copies, waits for them, and re-layouts  5.14 us (3%)
    ppermute x10, starting transfers between devices, chip_shift(): return lax.ppermute(array, 'line', pairs)  32 us
    pallas_call x7, Pallas kernels, call(): pl.pallas_call(kernel, out_shape=out_shape, in_specs=specs, out_specs=out...  23.6 us
    ppermute x8, waiting for transfers between devices, z_shift(): return lax.ppermute(array, 'span', pairs)  19.4 us
    pallas_call x2, Pallas kernels, chip_chain(): pl.pallas_call(chain_kernel(order), name='chain', grid_spec=pltpu.Prefetc...  14.5 us
    ppermute x8, starting transfers between devices, z_shift(): return lax.ppermute(array, 'span', pairs)  14.5 us
    ppermute x7, starting transfers between devices, core_swap(): return lax.ppermute(array, 'line', [(i, i ^ 1) for i in range(8)])  12.2 us
    ppermute x2, waiting for transfers between devices, y_shift_cross(): return lax.ppermute(array, ('line', 'span'), pairs)  10.7 us
    ppermute x10, waiting for transfers between devices, chip_shift(): return lax.ppermute(array, 'line', pairs)  10 us
  transfers between devices with their start and end apart: 33, of which 15 were waited for; matrix products, arithmetic and copies ran while one was open for 2% of the time, Pallas kernels for 18%

commit v1 on v0

--- a/solution.py
+++ b/solution.py
@@ -385,7 +385,7 @@
                 ],
             ),
             out_shape=[split_shape, split_shape, f32(2, 2, NB, ROW)],
-            compiler_params=pltpu.CompilerParams(vmem_limit_bytes=60 << 20),
+            compiler_params=pltpu.CompilerParams(vmem_limit_bytes=20 << 20),
             cost_estimate=pl.CostEstimate(
                 flops=48 * NB * NB * NV, bytes_accessed=64 * NB * NB, transcendentals=0
             ),
@@ -402,32 +402,33 @@
     lower_came = core_swap(lower_blocks)
     upper_came = core_swap(upper_blocks)
     lift = high_low(lift_operator.T)
-    l_split, up_all = chip_chain(lower_blocks, lower_came, (3, 2, 1, 0))
     asked = (neighbour_line * FACES + neighbour_face).reshape(1, SLOTS)
     table = jnp.concatenate([asked, y_shift(asked, -1)])
-    up1, down1, l_split, up_all, upper_came, table, lift = lax.optimization_barrier(
-        (up1, down1, l_split, up_all, upper_came, table, lift)
+    up1, down1, lower_came, table, lift = lax.optimization_barrier(
+        (up1, down1, lower_came, table, lift)
     )
     up2 = z_shift(up1, 1)
     down2 = z_shift(down1, -1)
+    l_split, up_all = chip_chain(lower_blocks, lower_came, (3, 2, 1, 0))
     m1 = chip_shift(up_all, 1, (1, 2))
     m2 = chip_shift(up_all, 2, (1,))
     pivot_came = core_swap(pivot_inverse)
     residual_came = core_swap(residual)
     jacobian_came = core_swap(flux_jacobian)
+    up2, down2, l_split, up_all, upper_came, pivot_came, residual_came, jacobian_came = (
+        lax.optimization_barrier(
+            (up2, down2, l_split, up_all, upper_came, pivot_came, residual_came, jacobian_came)
+        )
+    )
+    up3 = z_shift(up2, 1)
+    down3 = z_shift(down2, -1)
     u_split, down_all = chip_chain(upper_blocks, upper_came, (0, 1, 2, 3))
     n1 = chip_shift(down_all, -1, (2, 1))
     n2 = chip_shift(down_all, -2, (2,))
-    up2, down2, u_split, down_all, pivot_came, residual_came, jacobian_came = (
-        lax.optimization_barrier(
-            (up2, down2, u_split, down_all, pivot_came, residual_came, jacobian_came)
-        )
-    )
-    up3 = z_shift(up2, 1)
-    down3 = z_shift(down2, -1)
-    pivot = pivot_parts(pivot_came, residual_came)
     table = jnp.concatenate([table, y_shift(table, 2)])
-    up3, down3, table, pivot = lax.optimization_barrier((up3, down3, table, pivot))
+    up3, down3, table, u_split, down_all = lax.optimization_barrier(
+        (up3, down3, table, u_split, down_all)
+    )
     up_half, down_half = call(
         halves_kernel, [VMEM] * 2, [f32(HALF, NF, ROW)] * 2, (up3, down3), 0, mib=4
     )
@@ -452,6 +453,8 @@
     next_own, prev_other = pick(((1, False, YS - 1), (3, True, 1)), (far, far_other))
     below = y_shift(next_own, 1)
     above_cross = y_shift_cross(prev_other, -1)
+    pivot_came, next_own = lax.optimization_barrier((pivot_came, next_own))
+    pivot = pivot_parts(pivot_came, residual_came)
     mine, mine_other = pick(((0, False, 0), (0, True, 0)))
     mine_cross = core_swap(mine_other)
 
@@ -464,13 +467,14 @@
         [pltpu.VMEM((NB, ROW), jnp.float32), pltpu.VMEM((2, 2, NB, ROW), jnp.float32)],
         mib=24,
     )
-    driving, last, m1, m2, n1, n2 = lax.optimization_barrier((driving, last, m1, m2, n1, n2))
+    driving, last, m1, m2 = lax.optimization_barrier((driving, last, m1, m2))
     split_scratch = [pltpu.VMEM((2, NB, NB), jnp.bfloat16)] * 4
     sweep, first = call(
         middle_kernel, [SMEM] + [VMEM] * 10, [f32(4, NB, ROW), f32(NB, ROW)],
         (alive, chip_shift(last, 1), chip_shift(last, 2), chip_shift(last, 3),
          m1, m2, driving, *l_split, *u_split), 18 * matmul, split_scratch, mib=24,
     )
+    sweep, first, n1, n2 = lax.optimization_barrier((sweep, first, n1, n2))
     kept, sent = call(
         backward_kernel, [SMEM] * 2 + [VMEM] * 8, [f32(2, 2, NV, NB)] * 2,
         (core_ref, alive, chip_shift(first, -1), chip_shift(first, -2), chip_shift(first, -3),

time: 175 us -> 172 us (0.983)
  starting transfers between devices: 71.9 us -> 56.1 us
  waiting for transfers between devices: 48 us -> 59.2 us
    ppermute x10, starting transfers between devices: 32 us -> 16.7 us  [chip_shift(): return lax.ppermute(array, 'line', pairs)]
    ppermute x2, starting transfers between devices: 9.29 us -> 0.44 us  [y_shift_cross(): return lax.ppermute(array, ('line', 'span'), pairs)]
    ppermute x8, waiting for transfers between devices: 19.4 us -> 26 us  [z_shift(): return lax.ppermute(array, 'span', pairs)]
    ppermute x6, starting transfers between devices: 3.89 us -> 9.74 us  [y_shift(): return lax.ppermute(array, 'span', pairs)]
    ppermute x7, starting transfers between devices: 12.2 us -> 16 us  [core_swap(): return lax.ppermute(array, 'line', [(i, i ^ 1) for i in range(8)])]
    ppermute x10, waiting for transfers between devices: 10 us -> 12.2 us  [chip_shift(): return lax.ppermute(array, 'line', pairs)]
  transfers between devices with their start and end apart: 33 -> 33, of which waited for: 15 -> 18; matrix products, arithmetic and copies ran while one was open for 2% -> 3% of each run, Pallas kernels for 18% -> 20%
where the time goes in v1:
time: 172 us; the launch traced here: 171 us
  waiting for transfers between devices  59.2 us (34%)
  starting transfers between devices  56.1 us (33%)
  Pallas kernels  42 us (24%)
  other arithmetic  6.31 us (4%)
  local copies, waits for them, and re-layouts  6.15 us (4%)
    ppermute x8, waiting for transfers between devices, z_shift(): return lax.ppermute(array, 'span', pairs)  26 us
    pallas_call x7, Pallas kernels, call(): pl.pallas_call(kernel, out_shape=out_shape, in_specs=specs, out_specs=out...  23.7 us
    ppermute x10, starting transfers between devices, chip_shift(): return lax.ppermute(array, 'line', pairs)  16.7 us
    ppermute x7, starting transfers between devices, core_swap(): return lax.ppermute(array, 'line', [(i, i ^ 1) for i in range(8)])  16 us
    pallas_call x2, Pallas kernels, chip_chain(): pl.pallas_call(chain_kernel(order), name='chain', grid_spec=pltpu.Prefetc...  14.5 us
    ppermute x8, starting transfers between devices, z_shift(): return lax.ppermute(array, 'span', pairs)  13.2 us
    ppermute x10, waiting for transfers between devices, chip_shift(): return lax.ppermute(array, 'line', pairs)  12.2 us
    ppermute x2, waiting for transfers between devices, y_shift_cross(): return lax.ppermute(array, ('line', 'span'), pairs)  11.9 us
  transfers between devices with their start and end apart: 33, of which 18 were waited for; matrix products, arithmetic and copies ran while one was open for 3% of the time, Pallas kernels for 20%

profile of v1, /device:TPU:1, one launch (start us, length us, event | category | flops | bytes accessed | tf_op | source)
XLA Modules:
  0.0 170.9 jit_solution(4989762185440742331)
XLA Ops:
  0.0 0.8 compare_convert_fusion
  0.8 1.3 broadcast_multiply_fusion
  2.1 0.8 fusion.1
  2.8 3.3 %collective-permute-start.2 = (f32[4,2,320,320]{3,2,1,0:T(8,128)}, f32[4,2,320,320]{3,2,1,0:T(8,128)}, u32[]{:S(2)}, u32[]{:S(2)}) collective-permute-start(f32[4,2,320,320]{3,2,1,0:T(8,128)} %kept), channel_id=1, source_target_pairs={{0,32},{32,0},{64,96},{96,64},{128,160},{160,128},{192,224},{224,1... | collective-permute-start | bytes 9830408 | tf_op jit(solution)/shard_map/ppermute | solution.py:50
  6.6 0.7 multiply_add_fusion
  7.4 2.7 %collective-permute-start.3 = (s32[1,16]{1,0:T(1,128)S(1)}, s32[1,16]{1,0:T(1,128)S(1)}, u32[]{:S(2)}, u32[]{:S(2)}) collective-permute-start(s32[1,16]{1,0:T(1,128)S(1)} %reshape.71), channel_id=1, source_target_pairs={{0,24},{1,25},{2,26},{3,27},{4,28},{5,29},{6,30},{7,31},{8,0},{9,1... | collective-permute-start | bytes 200 | tf_op jit(solution)/shard_map/ppermute | solution.py:35
  10.1 0.7 collective-permute-done.3
  10.8 3.9 %collective-permute-start.1 = (f32[16,80,128]{2,1,0:T(8,128)S(1)}, f32[16,80,128]{2,1,0:T(8,128)S(1)}, u32[]{:S(2)}, u32[]{:S(2)}) collective-permute-start(f32[16,80,128]{2,1,0:T(8,128)S(1)} %bitcast.21), channel_id=1, source_target_pairs={{0,7},{1,0},{2,1},{3,2},{4,3},{5,4},{6,5},{7,6},{8,15},{9,8},{10,9... | collective-permute-start | bytes 1966088 | tf_op jit(solution)/shard_map/ppermute | solution.py:30
  14.7 10.8 %collective-permute-done.up1 = f32[16,80,128]{2,1,0:T(8,128)S(1)} collective-permute-done((f32[16,80,128]{2,1,0:T(8,128)S(1)}, f32[16,80,128]{2,1,0:T(8,128)S(1)}, u32[]{:S(2)}, u32[]{:S(2)}) %collective-permute-start) | collective-permute-done | bytes 655392 | tf_op jit(solution)/shard_map/ppermute | solution.py:30
  25.5 0.7 collective-permute-start.8
  26.2 2.0 %copy.14 = f32[320,320]{0,1:T(8,128)} copy(f32[320,320]{1,0:T(8,128)} %param.18) | data formatting | bytes 819200 | tf_op jit(solution)/shard_map/optimization_barrier | solution.py:396
  28.2 1.5 collective-permute-start.9
  29.7 1.9 %fusion = (bf16[320,320]{1,0:T(8,128)(2,1)}, bf16[320,320]{1,0:T(8,128)(2,1)}) fusion(f32[320,320]{0,1:T(8,128)} %copy.14), kind=kLoop, calls=%fused_computation.3 | loop fusion | flops 409600 | bytes 819200 | tf_op jit(solution)/shard_map/convert_element_type | solution.py:65
  31.7 0.9 copy-done.13
  32.6 3.4 %collective-permute-start.5 = (f32[16,80,128]{2,1,0:T(8,128)S(1)}, f32[16,80,128]{2,1,0:T(8,128)S(1)}, u32[]{:S(2)}, u32[]{:S(2)}) collective-permute-start(f32[16,80,128]{2,1,0:T(8,128)S(1)} %collective-permute-done.1.down1), channel_id=1, source_target_pairs={{0,7},{1,0},{2,1},{3,2},{4,3},{5,4},{6,5},{7,6},{8,15},{9,8},{10,9... | collective-permute-start | bytes 1966088 | tf_op jit(solution)/shard_map/ppermute | solution.py:30
  36.1 0.7 compare_convert_fusion.1.alive
  36.7 7.3 %chain.2 = (bf16[2,4,320,320]{3,2,1,0:T(8,128)(2,1)}, bf16[2,4,320,320]{3,2,1,0:T(8,128)(2,1)}, f32[2,320,320]{2,1,0:T(8,128)}) custom-call(s32[1]{0:T(128)} %bitcast.core, f32[2,4]{1,0:T(2,128)} %compare_convert_fusion.1.alive, f32[4,2,320,320]{3,2,1,0:T(8,128)} %kept, f32[4,2,320,320]{3,2,1,0:T(8,128)} %collective-permute-done.2.came), custom_call_target="tpu_custom_call" | custom-call | flops 1179648000 | bytes 3276800 | tf_op jit(solution)/shard_map/chain/pallas_call | solution.py:345
  44.0 6.0 %collective-permute-done.4.up2 = f32[16,80,128]{2,1,0:T(8,128)} collective-permute-done((f32[16,80,128]{2,1,0:T(8,128)S(1)}, f32[16,80,128]{2,1,0:T(8,128)}, u32[]{:S(2)}, u32[]{:S(2)}) %collective-permute-start.4) | collective-permute-done | bytes 655392 | tf_op jit(solution)/shard_map/ppermute | solution.py:30
  50.2 0.8 copy-done.7
  51.0 2.6 %collective-permute-start.10 = (f32[16,80,128]{2,1,0:T(8,128)}, f32[16,80,128]{2,1,0:T(8,128)S(1)}, u32[]{:S(2)}, u32[]{:S(2)}) collective-permute-start(f32[16,80,128]{2,1,0:T(8,128)} %collective-permute-done.4.up2), channel_id=1, source_target_pairs={{0,1},{1,2},{2,3},{3,4},{4,5},{5,6},{6,7},{7,0},{8,9},{9,10},{10,1... | collective-permute-start | bytes 1966088 | tf_op jit(solution)/shard_map/ppermute | solution.py:30
  53.6 0.5 collective-permute-start.11
  54.1 2.2 %collective-permute-start.12 = (s32[2,16]{1,0:T(2,128)S(1)}, s32[2,16]{1,0:T(2,128)S(1)}, u32[]{:S(2)}, u32[]{:S(2)}) collective-permute-start(s32[2,16]{1,0:T(2,128)S(1)} %pad_add_fusion.1), channel_id=1, source_target_pairs={{0,16},{1,17},{2,18},{3,19},{4,20},{5,21},{6,22},{7,23},{8,24},{9,... | collective-permute-start | bytes 392 | tf_op jit(solution)/shard_map/ppermute | solution.py:35
  56.3 1.8 %collective-permute-done.12 = s32[2,16]{1,0:T(2,128)S(1)} collective-permute-done((s32[2,16]{1,0:T(2,128)S(1)}, s32[2,16]{1,0:T(2,128)S(1)}, u32[]{:S(2)}, u32[]{:S(2)}) %collective-permute-start.12) | collective-permute-done | bytes 160 | tf_op jit(solution)/shard_map/ppermute | solution.py:35
  58.0 7.2 %chain.3 = (bf16[2,4,320,320]{3,2,1,0:T(8,128)(2,1)}, bf16[2,4,320,320]{3,2,1,0:T(8,128)(2,1)}, f32[2,320,320]{2,1,0:T(8,128)}) custom-call(s32[1]{0:T(128)} %bitcast.core, f32[2,4]{1,0:T(2,128)} %compare_convert_fusion.1.alive, f32[4,2,320,320]{3,2,1,0:T(8,128)} %kept.1, f32[4,2,320,320]{3,2,1,0:T(8,128)} %collective-permute-done.6.came), custom_call_target="tpu_custom_call" | custom-call | flops 1179648000 | bytes 3276800 | tf_op jit(solution)/shard_map/chain/pallas_call | solution.py:345
  65.3 3.0 %collective-permute-done.10.up.up3 = f32[16,80,128]{2,1,0:T(8,128)S(1)} collective-permute-done((f32[16,80,128]{2,1,0:T(8,128)}, f32[16,80,128]{2,1,0:T(8,128)S(1)}, u32[]{:S(2)}, u32[]{:S(2)}) %collective-permute-start.10) | collective-permute-done | bytes 655392 | tf_op jit(solution)/shard_map/ppermute | solution.py:30
  68.7 0.9 shard_map.109
  69.6 1.0 collective-permute-start.13
  70.6 1.7 collective-permute-start.14
  72.4 5.7 %collective-permute-done.13.up4 = f32[8,80,128]{2,1,0:T(8,128)S(1)} collective-permute-done((f32[8,80,128]{2,1,0:T(8,128)}, f32[8,80,128]{2,1,0:T(8,128)S(1)}, u32[]{:S(2)}, u32[]{:S(2)}) %collective-permute-start.13) | collective-permute-done | bytes 327712 | tf_op jit(solution)/shard_map/ppermute | solution.py:30
  78.1 1.1 copy-done.6
  79.2 1.1 copy-done.8
  80.3 2.4 %shard_map.111 = (f32[8,80,128]{2,1,0:T(8,128)S(1)}, f32[8,80,128]{2,1,0:T(8,128)S(1)}, f32[8,80,128]{2,1,0:T(8,128)S(1)}, f32[8,80,128]{2,1,0:T(8,128)S(1)}) custom-call(s32[4,16]{1,0:T(4,128)S(1)} %pad_add_fusion.table, s32[3]{0:T(128)S(1)} %pad_add_fusion.2.place, f32[16,80,128]{2,1,0:T(8,128)S(1)} %bitcast.22, ...), custom_call_target="tpu_custom_call" | custom-call | bytes 6553868 | tf_op jit(solution)/shard_map/pallas_call | solution.py:299
  82.6 0.7 collective-permute-start.15
  83.4 2.7 %collective-permute-start.16 = (f32[8,80,128]{2,1,0:T(8,128)S(1)}, f32[8,80,128]{2,1,0:T(8,128)S(1)}, u32[]{:S(2)}, u32[]{:S(2)}) collective-permute-start(f32[8,80,128]{2,1,0:T(8,128)S(1)} %get-tuple-element.96), channel_id=1, source_target_pairs={{0,24},{1,25},{2,26},{3,27},{4,28},{5,29},{6,30},{7,31},{8,0},{9,1... | collective-permute-start | bytes 983048 | tf_op jit(solution)/shard_map/ppermute | solution.py:35
  86.1 1.4 collective-permute-start.18
  87.5 2.0 %shard_map.110 = (f32[8,80,128]{2,1,0:T(8,128)S(1)}, f32[8,80,128]{2,1,0:T(8,128)S(1)}) custom-call(s32[4,16]{1,0:T(4,128)S(1)} %pad_add_fusion.table, s32[3]{0:T(128)S(1)} %pad_add_fusion.2.place, f32[16,80,128]{2,1,0:T(8,128)S(1)} %bitcast.23, f32[16,80,128]{2,1,0:T(8,128)S(1)} %collective-permute-done.up1, f32[16,80,128]{2,1,0:T(8,128)} %collective-permute-done.4.up2, ...), custom_call_target="tpu_custom_call" | custom-call | bytes 5898508 | tf_op jit(solution)/shard_map/pallas_call | solution.py:299
  89.5 4.2 %collective-permute-start.19 = (f32[8,80,128]{2,1,0:T(8,128)S(1)}, f32[8,80,128]{2,1,0:T(8,128)S(1)}, u32[]{:S(2)}, u32[]{:S(2)}) collective-permute-start(f32[8,80,128]{2,1,0:T(8,128)S(1)} %get-tuple-element.99), channel_id=1, source_target_pairs={{0,32},{32,0},{64,96},{96,64},{128,160},{160,128},{192,224},{224,1... | collective-permute-start | bytes 983048 | tf_op jit(solution)/shard_map/ppermute | solution.py:50
  93.6 2.0 %shard_map.112 = (f32[8,80,128]{2,1,0:T(8,128)S(1)}, f32[8,80,128]{2,1,0:T(8,128)S(1)}) custom-call(s32[4,16]{1,0:T(4,128)S(1)} %pad_add_fusion.table, s32[3]{0:T(128)S(1)} %pad_add_fusion.2.place, f32[16,80,128]{2,1,0:T(8,128)S(1)} %bitcast.24, f32[16,80,128]{2,1,0:T(8,128)S(1)} %collective-permute-done.up1, f32[16,80,128]{2,1,0:T(8,128)} %collective-permute-done.4.up2, ...), custom_call_target="tpu_custom_call" | custom-call | bytes 6553868 | tf_op jit(solution)/shard_map/pallas_call | solution.py:299
  95.7 0.7 collective-permute-start.22
  96.5 0.5 collective-permute-done.18.above
  96.9 0.7 collective-permute-start.23
  97.7 1.3 collective-permute-start.27
  99.0 5.9 %collective-permute-done.20.below_cross = f32[8,80,128]{2,1,0:T(8,128)S(1)} collective-permute-done((f32[8,80,128]{2,1,0:T(8,128)S(1)}, f32[8,80,128]{2,1,0:T(8,128)S(1)}, u32[]{:S(2)}, u32[]{:S(2)}) %collective-permute-start.20) | collective-permute-done | bytes 327712 | tf_op jit(solution)/shard_map/ppermute | solution.py:46
  104.8 1.3 collective-permute-start.28
  106.1 4.8 %collective-permute-done.17.below = f32[8,80,128]{2,1,0:T(8,128)S(1)} collective-permute-done((f32[8,80,128]{2,1,0:T(8,128)S(1)}, f32[8,80,128]{2,1,0:T(8,128)S(1)}, u32[]{:S(2)}, u32[]{:S(2)}) %collective-permute-start.17) | collective-permute-done | bytes 327712 | tf_op jit(solution)/shard_map/ppermute | solution.py:35
  111.4 3.8 %own.1 = (bf16[2,4,320,320]{3,2,1,0:T(8,128)(2,1)S(1)}, bf16[2,4,320,320]{3,2,1,0:T(8,128)(2,1)S(1)}, f32[2,2,320,128]{3,2,1,0:T(8,128)S(1)}) custom-call(s32[1]{0:T(128)} %bitcast.core, f32[4,2,320,320]{3,2,1,0:T(8,128)S(1)} %copy-done.9, f32[4,2,320,320]{3,2,1,0:T(8,128)} %collective-permute-done.7.came, f32[4,2,64,320]{3,2,1,0:T(8,128)S(1)} %copy-done.12, ...), custom_call_target="tpu_custom_call" | custom-call | flops 314572800 | bytes 6553600 | tf_op jit(solution)/shard_map/own/pallas_call | solution.py:374
  115.2 6.0 %collective-permute-done.21.above_cross = f32[8,80,128]{2,1,0:T(8,128)S(1)} collective-permute-done((f32[8,80,128]{2,1,0:T(8,128)S(1)}, f32[8,80,128]{2,1,0:T(8,128)S(1)}, u32[]{:S(2)}, u32[]{:S(2)}) %collective-permute-start.21) | collective-permute-done | bytes 327712 | tf_op jit(solution)/shard_map/ppermute | solution.py:46
  121.3 7.9 %shard_map.113 = (f32[4,320,128]{2,1,0:T(8,128)S(1)}, f32[320,128]{1,0:T(8,128)S(1)}) custom-call(s32[4,16]{1,0:T(4,128)S(1)} %pad_add_fusion.table, s32[3]{0:T(128)S(1)} %pad_add_fusion.2.place, f32[2,4]{1,0:T(2,128)S(1)} %copy-done.15, f32[8,80,128]{2,1,0:T(8,128)S(1)} %get-tuple-element.94.mine, f32[8,80,128]{2,1,0:T(8,128)S(1)} %collective-permute-done.17.below, ...), custom_call_target="tpu_custom_call" | custom-call | flops 2044723200 | bytes 19005740 | tf_op jit(solution)/shard_map/pallas_call | solution.py:299
  129.2 3.1 %collective-permute-start.24 = (f32[320,128]{1,0:T(8,128)S(1)}, f32[320,128]{1,0:T(8,128)S(1)}, u32[]{:S(2)}, u32[]{:S(2)}) collective-permute-start(f32[320,128]{1,0:T(8,128)S(1)} %get-tuple-element.115), channel_id=1, source_target_pairs={{0,64},{32,96},{64,128},{96,160},{128,192},{160,224},{1,65},{33,97... | collective-permute-start | bytes 491528 | tf_op jit(solution)/shard_map/ppermute | solution.py:60
  132.4 4.4 %collective-permute-start.25 = (f32[320,128]{1,0:T(8,128)S(1)}, f32[320,128]{1,0:T(8,128)S(1)}, u32[]{:S(2)}, u32[]{:S(2)}) collective-permute-start(f32[320,128]{1,0:T(8,128)S(1)} %get-tuple-element.115), channel_id=1, source_target_pairs={{0,128},{32,160},{64,192},{96,224},{1,129},{33,161},{65,193},{97,2... | collective-permute-start | bytes 491528 | tf_op jit(solution)/shard_map/ppermute | solution.py:60
  136.7 1.3 collective-permute-start.26
  138.0 0.9 collective-permute-done.25.mid
  139.0 3.5 %collective-permute-done.26.far = f32[320,128]{1,0:T(8,128)S(1)} collective-permute-done((f32[320,128]{1,0:T(8,128)S(1)}, f32[320,128]{1,0:T(8,128)S(1)}, u32[]{:S(2)}, u32[]{:S(2)}) %collective-permute-start.26) | collective-permute-done | bytes 163872 | tf_op jit(solution)/shard_map/ppermute | solution.py:60
  142.5 4.8 %shard_map.114 = (f32[4,320,128]{2,1,0:T(8,128)S(1)}, f32[320,128]{1,0:T(8,128)S(1)}) custom-call(f32[2,4]{1,0:T(2,128)S(1)} %copy-done.15, f32[320,128]{1,0:T(8,128)S(1)} %collective-permute-done.24.near, f32[320,128]{1,0:T(8,128)S(1)} %collective-permute-done.25.mid, f32[320,128]{1,0:T(8,128)S(1)} %collective-permute-done.26.far, ...), custom_call_target="tpu_custom_call" | custom-call | flops 1415577600 | bytes 16711712 | tf_op jit(solution)/shard_map/pallas_call | solution.py:299
  147.2 1.3 collective-permute-start.29
  148.5 1.3 collective-permute-start.30
  149.8 1.3 collective-permute-start.31
  151.1 2.2 %collective-permute-done.29.near = f32[320,128]{1,0:T(8,128)S(1)} collective-permute-done((f32[320,128]{1,0:T(8,128)S(1)}, f32[320,128]{1,0:T(8,128)S(1)}, u32[]{:S(2)}, u32[]{:S(2)}) %collective-permute-start.29) | collective-permute-done | bytes 163872 | tf_op jit(solution)/shard_map/ppermute | solution.py:60
  153.3 2.8 %collective-permute-done.30.mid = f32[320,128]{1,0:T(8,128)S(1)} collective-permute-done((f32[320,128]{1,0:T(8,128)S(1)}, f32[320,128]{1,0:T(8,128)S(1)}, u32[]{:S(2)}, u32[]{:S(2)}) %collective-permute-start.30) | collective-permute-done | bytes 163872 | tf_op jit(solution)/shard_map/ppermute | solution.py:60
  156.1 2.8 %collective-permute-done.31.far = f32[320,128]{1,0:T(8,128)S(1)} collective-permute-done((f32[320,128]{1,0:T(8,128)S(1)}, f32[320,128]{1,0:T(8,128)S(1)}, u32[]{:S(2)}, u32[]{:S(2)}) %collective-permute-start.31) | collective-permute-done | bytes 163872 | tf_op jit(solution)/shard_map/ppermute | solution.py:60
  158.9 3.8 %shard_map.115 = (f32[2,2,64,320]{3,2,1,0:T(8,128)S(1)}, f32[2,2,64,320]{3,2,1,0:T(8,128)S(1)}) custom-call(s32[1]{0:T(128)} %bitcast.core, f32[2,4]{1,0:T(2,128)S(1)} %copy-done.15, f32[320,128]{1,0:T(8,128)S(1)} %collective-permute-done.29.near, f32[320,128]{1,0:T(8,128)S(1)} %collective-permute-done.30.mid, f32[320,128]{1,0:T(8,128)S(1)} %collective-permute-done.31.far, ...), custom_call_target="tpu_custom_call" | custom-call | flops 943718400 | bytes 9994276 | tf_op jit(solution)/shard_map/pallas_call | solution.py:299
  162.7 5.9 %collective-permute-start.32 = (f32[2,2,64,320]{3,2,1,0:T(8,128)S(1)}, f32[2,2,64,320]{3,2,1,0:T(8,128)S(1)}, u32[]{:S(2)}, u32[]{:S(2)}) collective-permute-start(f32[2,2,64,320]{3,2,1,0:T(8,128)S(1)} %get-tuple-element.128), channel_id=1, source_target_pairs={{0,32},{32,0},{64,96},{96,64},{128,160},{160,128},{192,224},{224,1... | collective-permute-start | bytes 983048 | tf_op jit(solution)/shard_map/ppermute | solution.py:50
  168.6 1.3 collective-permute-done.32
  170.0 0.9 maximum_select_fusion
  (65 shorter events, 2.0 us)
Async XLA Ops:
  0.0 2.1 %copy-start = (f32[320,320]{1,0:T(8,128)S(1)}, f32[320,320]{1,0:T(8,128)}, u32[]{:S(2)}) copy-start(f32[320,320]{1,0:T(8,128)} %param.17) | copy-start | bytes 1228804
  0.0 36.0 %copy-start.16 = (s32[4]{0:T(128)S(1)}, s32[4]{0:T(128)}, u32[]{:S(2)}) copy-start(s32[4]{0:T(128)} %param.19) | copy-start | bytes 52
  2.8 28.8 %collective-permute-start.2 = (f32[4,2,320,320]{3,2,1,0:T(8,128)}, f32[4,2,320,320]{3,2,1,0:T(8,128)}, u32[]{:S(2)}, u32[]{:S(2)}) collective-permute-start(f32[4,2,320,320]{3,2,1,0:T(8,128)} %kept), channel_id=1, source_target_pairs={{0,32},{32,0},{64,96},{96,64},{128,160},{160,128},{192,224},{224,1... | collective-permute-start | bytes 9830408 | tf_op jit(solution)/shard_map/ppermute | solution.py:50
  6.1 37.9 %collective-permute-start.6 = (f32[4,2,320,320]{3,2,1,0:T(8,128)}, f32[4,2,320,320]{3,2,1,0:T(8,128)}, u32[]{:S(2)}, u32[]{:S(2)}) collective-permute-start(f32[4,2,320,320]{3,2,1,0:T(8,128)} %kept.1), channel_id=1, source_target_pairs={{0,32},{32,0},{64,96},{96,64},{128,160},{160,128},{192,224},{224,1... | collective-permute-start | bytes 9830408 | tf_op jit(solution)/shard_map/ppermute | solution.py:50
  6.2 37.8 %collective-permute-start.7 = (f32[4,2,320,320]{3,2,1,0:T(8,128)}, f32[4,2,320,320]{3,2,1,0:T(8,128)}, u32[]{:S(2)}, u32[]{:S(2)}) collective-permute-start(f32[4,2,320,320]{3,2,1,0:T(8,128)} %kept.2), channel_id=1, source_target_pairs={{0,32},{32,0},{64,96},{96,64},{128,160},{160,128},{192,224},{224,1... | collective-permute-start | bytes 9830408 | tf_op jit(solution)/shard_map/ppermute | solution.py:50
  6.6 18.9 %collective-permute-start = (f32[16,80,128]{2,1,0:T(8,128)S(1)}, f32[16,80,128]{2,1,0:T(8,128)S(1)}, u32[]{:S(2)}, u32[]{:S(2)}) collective-permute-start(f32[16,80,128]{2,1,0:T(8,128)S(1)} %bitcast.20), channel_id=1, source_target_pairs={{0,1},{1,2},{2,3},{3,4},{4,5},{5,6},{6,7},{7,0},{8,9},{9,10},{10,1... | collective-permute-start | bytes 1966088 | tf_op jit(solution)/shard_map/ppermute | solution.py:30
  7.4 3.4 %collective-permute-start.3 = (s32[1,16]{1,0:T(1,128)S(1)}, s32[1,16]{1,0:T(1,128)S(1)}, u32[]{:S(2)}, u32[]{:S(2)}) collective-permute-start(s32[1,16]{1,0:T(1,128)S(1)} %reshape.71), channel_id=1, source_target_pairs={{0,24},{1,25},{2,26},{3,27},{4,28},{5,29},{6,30},{7,31},{8,0},{9,1... | collective-permute-start | bytes 200 | tf_op jit(solution)/shard_map/ppermute | solution.py:35
  10.8 17.4 %collective-permute-start.1 = (f32[16,80,128]{2,1,0:T(8,128)S(1)}, f32[16,80,128]{2,1,0:T(8,128)S(1)}, u32[]{:S(2)}, u32[]{:S(2)}) collective-permute-start(f32[16,80,128]{2,1,0:T(8,128)S(1)} %bitcast.21), channel_id=1, source_target_pairs={{0,7},{1,0},{2,1},{3,2},{4,3},{5,4},{6,5},{7,6},{8,15},{9,8},{10,9... | collective-permute-start | bytes 1966088 | tf_op jit(solution)/shard_map/ppermute | solution.py:30
  25.5 6.2 %collective-permute-start.8 = (f32[4,2,64,320]{3,2,1,0:T(8,128)}, f32[4,2,64,320]{3,2,1,0:T(8,128)S(1)}, u32[]{:S(2)}, u32[]{:S(2)}) collective-permute-start(f32[4,2,64,320]{3,2,1,0:T(8,128)} %given_kept), channel_id=1, source_target_pairs={{0,32},{32,0},{64,96},{96,64},{128,160},{160,128},{192,224},{224,1... | collective-permute-start | bytes 1966088 | tf_op jit(solution)/shard_map/ppermute | solution.py:50
  28.2 15.8 %copy-start.5 = (f32[16,80,128]{2,1,0:T(8,128)}, f32[16,80,128]{2,1,0:T(8,128)S(1)}, u32[]{:S(2)}) copy-start(f32[16,80,128]{2,1,0:T(8,128)S(1)} %collective-permute-done.1.down1) | copy-start | bytes 1966084
  28.2 15.8 %collective-permute-start.9 = (f32[4,2,80,320]{3,2,1,0:T(8,128)}, f32[4,2,80,320]{3,2,1,0:T(8,128)}, u32[]{:S(2)}, u32[]{:S(2)}) collective-permute-start(f32[4,2,80,320]{3,2,1,0:T(8,128)} %jacobian), channel_id=1, source_target_pairs={{0,32},{32,0},{64,96},{96,64},{128,160},{160,128},{192,224},{224,1... | collective-permute-start | bytes 2457608 | tf_op jit(solution)/shard_map/ppermute | solution.py:50
  31.6 18.5 %collective-permute-start.4 = (f32[16,80,128]{2,1,0:T(8,128)S(1)}, f32[16,80,128]{2,1,0:T(8,128)}, u32[]{:S(2)}, u32[]{:S(2)}) collective-permute-start(f32[16,80,128]{2,1,0:T(8,128)S(1)} %collective-permute-done.up1), channel_id=1, source_target_pairs={{0,1},{1,2},{2,3},{3,4},{4,5},{5,6},{6,7},{7,0},{8,9},{9,10},{10,1... | collective-permute-start | bytes 1966088 | tf_op jit(solution)/shard_map/ppermute | solution.py:30
  31.7 0.9 copy-start.13
  32.6 17.5 %collective-permute-start.5 = (f32[16,80,128]{2,1,0:T(8,128)S(1)}, f32[16,80,128]{2,1,0:T(8,128)S(1)}, u32[]{:S(2)}, u32[]{:S(2)}) collective-permute-start(f32[16,80,128]{2,1,0:T(8,128)S(1)} %collective-permute-done.1.down1), channel_id=1, source_target_pairs={{0,7},{1,0},{2,1},{3,2},{4,3},{5,4},{6,5},{7,6},{8,15},{9,8},{10,9... | collective-permute-start | bytes 1966088 | tf_op jit(solution)/shard_map/ppermute | solution.py:30
  50.2 0.8 copy-start.7
  51.0 17.3 %collective-permute-start.10 = (f32[16,80,128]{2,1,0:T(8,128)}, f32[16,80,128]{2,1,0:T(8,128)S(1)}, u32[]{:S(2)}, u32[]{:S(2)}) collective-permute-start(f32[16,80,128]{2,1,0:T(8,128)} %collective-permute-done.4.up2), channel_id=1, source_target_pairs={{0,1},{1,2},{2,3},{3,4},{4,5},{5,6},{6,7},{7,0},{8,9},{9,10},{10,1... | collective-permute-start | bytes 1966088 | tf_op jit(solution)/shard_map/ppermute | solution.py:30
  53.6 15.1 %collective-permute-start.11 = (f32[16,80,128]{2,1,0:T(8,128)}, f32[16,80,128]{2,1,0:T(8,128)S(1)}, u32[]{:S(2)}, u32[]{:S(2)}) collective-permute-start(f32[16,80,128]{2,1,0:T(8,128)} %copy-done.7), channel_id=1, source_target_pairs={{0,7},{1,0},{2,1},{3,2},{4,3},{5,4},{6,5},{7,6},{8,15},{9,8},{10,9... | collective-permute-start | bytes 1966088 | tf_op jit(solution)/shard_map/ppermute | solution.py:30
  54.1 3.9 %collective-permute-start.12 = (s32[2,16]{1,0:T(2,128)S(1)}, s32[2,16]{1,0:T(2,128)S(1)}, u32[]{:S(2)}, u32[]{:S(2)}) collective-permute-start(s32[2,16]{1,0:T(2,128)S(1)} %pad_add_fusion.1), channel_id=1, source_target_pairs={{0,16},{1,17},{2,18},{3,19},{4,20},{5,21},{6,22},{7,23},{8,24},{9,... | collective-permute-start | bytes 392 | tf_op jit(solution)/shard_map/ppermute | solution.py:35
  69.6 8.5 %collective-permute-start.13 = (f32[8,80,128]{2,1,0:T(8,128)}, f32[8,80,128]{2,1,0:T(8,128)S(1)}, u32[]{:S(2)}, u32[]{:S(2)}) collective-permute-start(f32[8,80,128]{2,1,0:T(8,128)} %get-tuple-element.92), channel_id=1, source_target_pairs={{0,1},{1,2},{2,3},{3,4},{4,5},{5,6},{6,7},{7,0},{8,9},{9,10},{10,1... | collective-permute-start | bytes 983048 | tf_op jit(solution)/shard_map/ppermute | solution.py:30
  70.6 7.5 %collective-permute-start.14 = (f32[8,80,128]{2,1,0:T(8,128)}, f32[8,80,128]{2,1,0:T(8,128)}, u32[]{:S(2)}, u32[]{:S(2)}) collective-permute-start(f32[8,80,128]{2,1,0:T(8,128)} %get-tuple-element.93), channel_id=1, source_target_pairs={{0,7},{1,0},{2,1},{3,2},{4,3},{5,4},{6,5},{7,6},{8,15},{9,8},{10,9... | collective-permute-start | bytes 983048 | tf_op jit(solution)/shard_map/ppermute | solution.py:30
  78.1 1.1 copy-start.6
  79.2 1.1 copy-start.8
  82.6 11.0 %collective-permute-start.15 = (f32[8,80,128]{2,1,0:T(8,128)S(1)}, f32[8,80,128]{2,1,0:T(8,128)S(1)}, u32[]{:S(2)}, u32[]{:S(2)}) collective-permute-start(f32[8,80,128]{2,1,0:T(8,128)S(1)} %get-tuple-element.95), channel_id=1, source_target_pairs={{0,8},{1,9},{2,10},{3,11},{4,12},{5,13},{6,14},{7,15},{8,16},{9,17... | collective-permute-start | bytes 983048 | tf_op jit(solution)/shard_map/ppermute | solution.py:35
  83.4 10.3 %collective-permute-start.16 = (f32[8,80,128]{2,1,0:T(8,128)S(1)}, f32[8,80,128]{2,1,0:T(8,128)S(1)}, u32[]{:S(2)}, u32[]{:S(2)}) collective-permute-start(f32[8,80,128]{2,1,0:T(8,128)S(1)} %get-tuple-element.96), channel_id=1, source_target_pairs={{0,24},{1,25},{2,26},{3,27},{4,28},{5,29},{6,30},{7,31},{8,0},{9,1... | collective-permute-start | bytes 983048 | tf_op jit(solution)/shard_map/ppermute | solution.py:35
  86.1 10.9 %collective-permute-start.18 = (f32[8,80,128]{2,1,0:T(8,128)S(1)}, f32[8,80,128]{2,1,0:T(8,128)S(1)}, u32[]{:S(2)}, u32[]{:S(2)}) collective-permute-start(f32[8,80,128]{2,1,0:T(8,128)S(1)} %get-tuple-element.98), channel_id=1, source_target_pairs={{0,24},{1,25},{2,26},{3,27},{4,28},{5,29},{6,30},{7,31},{8,0},{9,1... | collective-permute-start | bytes 983048 | tf_op jit(solution)/shard_map/ppermute | solution.py:35
  87.5 8.3 %copy-start.18 = (f32[2,320,320]{2,1,0:T(8,128)S(1)}, f32[2,320,320]{2,1,0:T(8,128)}, u32[]{:S(2)}) copy-start(f32[2,320,320]{2,1,0:T(8,128)} %get-tuple-element.77) | copy-start | bytes 2457604
  87.5 10.2 %copy-start.17 = (f32[2,320,320]{2,1,0:T(8,128)S(1)}, f32[2,320,320]{2,1,0:T(8,128)}, u32[]{:S(2)}) copy-start(f32[2,320,320]{2,1,0:T(8,128)} %get-tuple-element.88) | copy-start | bytes 2457604
  89.4 22.0 %copy-start.9 = (f32[4,2,320,320]{3,2,1,0:T(8,128)S(1)}, f32[4,2,320,320]{3,2,1,0:T(8,128)}, u32[]{:S(2)}) copy-start(f32[4,2,320,320]{3,2,1,0:T(8,128)} %kept.2) | copy-start | bytes 9830404
  89.4 22.0 %copy-start.12 = (f32[4,2,64,320]{3,2,1,0:T(8,128)S(1)}, f32[4,2,64,320]{3,2,1,0:T(8,128)}, u32[]{:S(2)}) copy-start(f32[4,2,64,320]{3,2,1,0:T(8,128)} %given_kept) | copy-start | bytes 1966084
  89.4 22.0 %copy-start.14 = (f32[4,2,64,320]{3,2,1,0:T(8,128)S(1)}, f32[4,2,64,320]{3,2,1,0:T(8,128)}, u32[]{:S(2)}) copy-start(f32[4,2,64,320]{3,2,1,0:T(8,128)} %copy-done.13) | copy-start | bytes 1966084
  89.5 8.2 %collective-permute-start.19 = (f32[8,80,128]{2,1,0:T(8,128)S(1)}, f32[8,80,128]{2,1,0:T(8,128)S(1)}, u32[]{:S(2)}, u32[]{:S(2)}) collective-permute-start(f32[8,80,128]{2,1,0:T(8,128)S(1)} %get-tuple-element.99), channel_id=1, source_target_pairs={{0,32},{32,0},{64,96},{96,64},{128,160},{160,128},{192,224},{224,1... | collective-permute-start | bytes 983048 | tf_op jit(solution)/shard_map/ppermute | solution.py:50
  93.6 11.2 %collective-permute-start.20 = (f32[8,80,128]{2,1,0:T(8,128)S(1)}, f32[8,80,128]{2,1,0:T(8,128)S(1)}, u32[]{:S(2)}, u32[]{:S(2)}) collective-permute-start(f32[8,80,128]{2,1,0:T(8,128)S(1)} %get-tuple-element.100), channel_id=1, source_target_pairs={{0,40},{1,41},{2,42},{3,43},{4,44},{5,45},{6,46},{7,47},{8,48},{9,... | collective-permute-start | bytes 983048 | tf_op jit(solution)/shard_map/ppermute | solution.py:46
  95.6 15.3 %collective-permute-start.17 = (f32[8,80,128]{2,1,0:T(8,128)S(1)}, f32[8,80,128]{2,1,0:T(8,128)S(1)}, u32[]{:S(2)}, u32[]{:S(2)}) collective-permute-start(f32[8,80,128]{2,1,0:T(8,128)S(1)} %get-tuple-element.97), channel_id=1, source_target_pairs={{0,8},{1,9},{2,10},{3,11},{4,12},{5,13},{6,14},{7,15},{8,16},{9,17... | collective-permute-start | bytes 983048 | tf_op jit(solution)/shard_map/ppermute | solution.py:35
  95.7 33.5 %collective-permute-start.22 = (f32[2,320,320]{2,1,0:T(8,128)S(1)}, f32[2,320,320]{2,1,0:T(8,128)S(1)}, u32[]{:S(2)}, u32[]{:S(2)}) collective-permute-start(f32[2,320,320]{2,1,0:T(8,128)S(1)} %copy-done.18), channel_id=1, source_target_pairs={{64,128},{96,160},{128,192},{160,224},{65,129},{97,161},{129,193},... | collective-permute-start | bytes 2457608 | tf_op jit(solution)/shard_map/ppermute | solution.py:60
  96.9 32.3 %collective-permute-start.23 = (f32[2,320,320]{2,1,0:T(8,128)S(1)}, f32[2,320,320]{2,1,0:T(8,128)S(1)}, u32[]{:S(2)}, u32[]{:S(2)}) collective-permute-start(f32[2,320,320]{2,1,0:T(8,128)S(1)} %copy-done.18), channel_id=1, source_target_pairs={{64,192},{96,224},{65,193},{97,225},{66,194},{98,226},{67,195},{99... | collective-permute-start | bytes 2457608 | tf_op jit(solution)/shard_map/ppermute | solution.py:60
  97.7 49.5 %collective-permute-start.27 = (f32[2,320,320]{2,1,0:T(8,128)S(1)}, f32[2,320,320]{2,1,0:T(8,128)S(1)}, u32[]{:S(2)}, u32[]{:S(2)}) collective-permute-start(f32[2,320,320]{2,1,0:T(8,128)S(1)} %copy-done.17), channel_id=1, source_target_pairs={{128,64},{160,96},{64,0},{96,32},{129,65},{161,97},{65,1},{97,33},... | collective-permute-start | bytes 2457608 | tf_op jit(solution)/shard_map/ppermute | solution.py:60
  104.8 42.4 %collective-permute-start.28 = (f32[2,320,320]{2,1,0:T(8,128)S(1)}, f32[2,320,320]{2,1,0:T(8,128)S(1)}, u32[]{:S(2)}, u32[]{:S(2)}) collective-permute-start(f32[2,320,320]{2,1,0:T(8,128)S(1)} %copy-done.17), channel_id=1, source_target_pairs={{128,0},{160,32},{129,1},{161,33},{130,2},{162,34},{131,3},{163,35... | collective-permute-start | bytes 2457608 | tf_op jit(solution)/shard_map/ppermute | solution.py:60
  111.0 10.3 %copy-start.1 = (bf16[2,4,320,320]{3,2,1,0:T(8,128)(2,1)S(1)}, bf16[2,4,320,320]{3,2,1,0:T(8,128)(2,1)}, u32[]{:S(2)}) copy-start(bf16[2,4,320,320]{3,2,1,0:T(8,128)(2,1)} %get-tuple-element.75) | copy-start | bytes 4915204
  111.0 10.3 %copy-start.2 = (bf16[2,4,320,320]{3,2,1,0:T(8,128)(2,1)S(1)}, bf16[2,4,320,320]{3,2,1,0:T(8,128)(2,1)}, u32[]{:S(2)}) copy-start(bf16[2,4,320,320]{3,2,1,0:T(8,128)(2,1)} %get-tuple-element.76) | copy-start | bytes 4915204
  111.0 10.3 %copy-start.10 = (bf16[320,320]{1,0:T(8,128)(2,1)S(1)}, bf16[320,320]{1,0:T(8,128)(2,1)}, u32[]{:S(2)}) copy-start(bf16[320,320]{1,0:T(8,128)(2,1)} %get-tuple-element.104.lift_low) | copy-start | bytes 614404
  111.0 10.3 %copy-start.11 = (bf16[320,320]{1,0:T(8,128)(2,1)S(1)}, bf16[320,320]{1,0:T(8,128)(2,1)}, u32[]{:S(2)}) copy-start(bf16[320,320]{1,0:T(8,128)(2,1)} %get-tuple-element.103.lift_high) | copy-start | bytes 614404
  111.0 10.3 %copy-start.15 = (f32[2,4]{1,0:T(2,128)S(1)}, f32[2,4]{1,0:T(2,128)}, u32[]{:S(2)}) copy-start(f32[2,4]{1,0:T(2,128)} %compare_convert_fusion.1.alive) | copy-start | bytes 100
  111.0 10.3 %collective-permute-start.21 = (f32[8,80,128]{2,1,0:T(8,128)S(1)}, f32[8,80,128]{2,1,0:T(8,128)S(1)}, u32[]{:S(2)}, u32[]{:S(2)}) collective-permute-start(f32[8,80,128]{2,1,0:T(8,128)S(1)} %get-tuple-element.101), channel_id=1, source_target_pairs={{0,56},{1,57},{2,58},{3,59},{4,60},{5,61},{6,62},{7,63},{8,32},{9,... | collective-permute-start | bytes 983048 | tf_op jit(solution)/shard_map/ppermute | solution.py:46
  121.3 21.2 %copy-start.3 = (bf16[2,4,320,320]{3,2,1,0:T(8,128)(2,1)S(1)}, bf16[2,4,320,320]{3,2,1,0:T(8,128)(2,1)}, u32[]{:S(2)}) copy-start(bf16[2,4,320,320]{3,2,1,0:T(8,128)(2,1)} %get-tuple-element.86) | copy-start | bytes 4915204
  121.3 21.2 %copy-start.4 = (bf16[2,4,320,320]{3,2,1,0:T(8,128)(2,1)S(1)}, bf16[2,4,320,320]{3,2,1,0:T(8,128)(2,1)}, u32[]{:S(2)}) copy-start(bf16[2,4,320,320]{3,2,1,0:T(8,128)(2,1)} %get-tuple-element.87) | copy-start | bytes 4915204
  129.2 8.8 %collective-permute-start.24 = (f32[320,128]{1,0:T(8,128)S(1)}, f32[320,128]{1,0:T(8,128)S(1)}, u32[]{:S(2)}, u32[]{:S(2)}) collective-permute-start(f32[320,128]{1,0:T(8,128)S(1)} %get-tuple-element.115), channel_id=1, source_target_pairs={{0,64},{32,96},{64,128},{96,160},{128,192},{160,224},{1,65},{33,97... | collective-permute-start | bytes 491528 | tf_op jit(solution)/shard_map/ppermute | solution.py:60
  132.4 6.6 %collective-permute-start.25 = (f32[320,128]{1,0:T(8,128)S(1)}, f32[320,128]{1,0:T(8,128)S(1)}, u32[]{:S(2)}, u32[]{:S(2)}) collective-permute-start(f32[320,128]{1,0:T(8,128)S(1)} %get-tuple-element.115), channel_id=1, source_target_pairs={{0,128},{32,160},{64,192},{96,224},{1,129},{33,161},{65,193},{97,2... | collective-permute-start | bytes 491528 | tf_op jit(solution)/shard_map/ppermute | solution.py:60
  136.7 5.7 %collective-permute-start.26 = (f32[320,128]{1,0:T(8,128)S(1)}, f32[320,128]{1,0:T(8,128)S(1)}, u32[]{:S(2)}, u32[]{:S(2)}) collective-permute-start(f32[320,128]{1,0:T(8,128)S(1)} %get-tuple-element.115), channel_id=1, source_target_pairs={{0,192},{32,224},{1,193},{33,225},{2,194},{34,226},{3,195},{35,227... | collective-permute-start | bytes 491528 | tf_op jit(solution)/shard_map/ppermute | solution.py:60
  147.2 6.1 %collective-permute-start.29 = (f32[320,128]{1,0:T(8,128)S(1)}, f32[320,128]{1,0:T(8,128)S(1)}, u32[]{:S(2)}, u32[]{:S(2)}) collective-permute-start(f32[320,128]{1,0:T(8,128)S(1)} %get-tuple-element.123), channel_id=1, source_target_pairs={{64,0},{96,32},{128,64},{160,96},{192,128},{224,160},{65,1},{97,33... | collective-permute-start | bytes 491528 | tf_op jit(solution)/shard_map/ppermute | solution.py:60
  148.5 7.6 %collective-permute-start.30 = (f32[320,128]{1,0:T(8,128)S(1)}, f32[320,128]{1,0:T(8,128)S(1)}, u32[]{:S(2)}, u32[]{:S(2)}) collective-permute-start(f32[320,128]{1,0:T(8,128)S(1)} %get-tuple-element.123), channel_id=1, source_target_pairs={{128,0},{160,32},{192,64},{224,96},{129,1},{161,33},{193,65},{225,... | collective-permute-start | bytes 491528 | tf_op jit(solution)/shard_map/ppermute | solution.py:60
  149.8 9.1 %collective-permute-start.31 = (f32[320,128]{1,0:T(8,128)S(1)}, f32[320,128]{1,0:T(8,128)S(1)}, u32[]{:S(2)}, u32[]{:S(2)}) collective-permute-start(f32[320,128]{1,0:T(8,128)S(1)} %get-tuple-element.123), channel_id=1, source_target_pairs={{192,0},{224,32},{193,1},{225,33},{194,2},{226,34},{195,3},{227,35... | collective-permute-start | bytes 491528 | tf_op jit(solution)/shard_map/ppermute | solution.py:60
  162.7 7.2 %collective-permute-start.32 = (f32[2,2,64,320]{3,2,1,0:T(8,128)S(1)}, f32[2,2,64,320]{3,2,1,0:T(8,128)S(1)}, u32[]{:S(2)}, u32[]{:S(2)}) collective-permute-start(f32[2,2,64,320]{3,2,1,0:T(8,128)S(1)} %get-tuple-element.128), channel_id=1, source_target_pairs={{0,32},{32,0},{64,96},{96,64},{128,160},{160,128},{192,224},{224,1... | collective-permute-start | bytes 983048 | tf_op jit(solution)/shard_map/ppermute | solution.py:50
